TPU v7x, 32 devices: a whole 2x2x4 slice. The times are simulated.
32 devices in a mesh: dp: 16 (over z, y, core), seq: 2 (over x).
Axes of the slice: x: 2, y: 2, z: 4, core: 2. Of those that a mesh axis runs over, the one named last changes fastest.
Arguments:
- x_in: bfloat16 [16, 256, 1024], P('dp', 'seq'), may hold values from -6 to 6
- cotangent: bfloat16 [16, 256, 1024], P('dp', 'seq'), may hold values from -6 to 6
- params: float32 [6602752], P(('dp', 'seq')), may hold values from -8 to 8
- moment_one: float32 [6602752], P(('dp', 'seq')), may hold values from -6 to 6
- moment_two: float32 [6602752], P(('dp', 'seq')), may hold values from 10 to 1000
Outputs:
- y_out: bfloat16 [16, 256, 1024], P('dp', 'seq')
- input_grad: bfloat16 [16, 256, 1024], P('dp', 'seq')
- weight_grads: float32 [6602752], P(('dp', 'seq'))
- new_params: float32 [6602752], P(('dp', 'seq'))
- new_moment_one: float32 [6602752], P(('dp', 'seq'))
- new_moment_two: float32 [6602752], P(('dp', 'seq'))
All inputs are finite; a program needn't handle non-finite values.
Results may differ from a plain program's by a relative error of at most 0.012.
Values may be sent and summed in bfloat16 or wider, within the bound.
No kernel may reach another device: no remote copies, remote signals or barrier semaphores. Data moves between devices by JAX's collectives and lax.ppermute only.
A program may use at most 192 MiB of HBM per device.

v0:
```python
import functools
import jax
import jax.numpy as jnp
import numpy as np
from jax import lax
from jax.experimental import pallas as pl
from jax.experimental.pallas import tpu as pltpu
from jax.sharding import PartitionSpec as P

D = 1024
DI = 2048
N = 128
K = 4
SPAN = 128
H = 32
CONV = 2304
PROJ = 4384
WIDE = 4480
IN = D * PROJ
OUT = DI * D
SMALL = K * CONV + CONV + D + DI + 3 * H

norm_eps = 1e-05
learn_rate = 0.005
beta_one = 0.9
beta_two = 0.95
adam_eps = 1e-08
weight_decay = 0.1
adam_step = 10

bf16 = jnp.bfloat16
f32 = jnp.float32


def ceil_to(value, unit):
    return -(-value // unit) * unit


def factors(count):
    core = 2 if count % 2 == 0 else 1
    rest = count // core
    mid = 1
    while rest % (mid * 2) == 0 and (mid * 2) ** 2 <= rest * 1:
        mid *= 2
    return rest // mid, mid, core


def dot(a, b, dims=((1,), (0,))):
    return lax.dot_general(a, b, (dims, ((), ())), preferred_element_type=f32)


def col_roll(a, steps):
    rows = a.shape[0]
    at = lax.broadcasted_iota(jnp.int32, a.shape, 0)
    if steps >= 0:
        return jnp.where(at >= steps, pltpu.roll(a, steps, 0), 0.0)
    return jnp.where(at < rows + steps, pltpu.roll(a, rows + steps, 0), 0.0)


def conv_act(x, taps, bias):
    acc = bias + taps[K - 1 : K] * x
    for k in range(1, K):
        acc = acc + taps[K - 1 - k : K - k] * col_roll(x, k)
    sig = 1.0 / (1.0 + jnp.exp(-acc))
    return acc, sig


def conv_back(x, taps, d_acc):
    d_x = taps[K - 1 : K] * d_acc
    d_taps = [jnp.sum(d_acc * x, axis=0, keepdims=True)]
    for k in range(1, K):
        d_x = d_x + taps[K - 1 - k : K - k] * col_roll(d_acc, -k)
        d_taps.insert(0, jnp.sum(d_acc * col_roll(x, k), axis=0, keepdims=True))
    return d_x, d_taps, jnp.sum(d_acc, axis=0, keepdims=True)


def fine(a, b, dims):
    return lax.dot_general(
        a, b, (dims, ((), ())), precision=lax.Precision.HIGHEST, preferred_element_type=f32
    )


def tri_parts():
    row = lax.broadcasted_iota(jnp.int32, (SPAN, SPAN), 0)
    col = lax.broadcasted_iota(jnp.int32, (SPAN, SPAN), 1)
    return row >= col, row == col


def rates(c, step_ref, turn_ref, alog_ref, alog_turn_ref, lower):
    span = slice(c * SPAN, (c + 1) * SPAN)
    rate = step_ref[span, :] * -jnp.exp(alog_ref[...])
    rate_turn = turn_ref[:, span] * -jnp.exp(alog_turn_ref[...])
    within = fine(lower, rate, ((1,), (0,)))
    within_turn = fine(rate_turn, lower, ((1,), (1,)))
    return rate, within, within_turn


def lanes_of(pair, first, second):
    lane = lax.broadcasted_iota(jnp.int32, (1, 2 * pair), 1)
    return jnp.where(lane < pair, first, second)


def ssd_forward_kernel(
    hsize, x_ref, bc_ref, wx_ref, bx_ref, wb_ref, bb_ref, step_ref, turn_ref, alog_ref, alog_turn_ref, skip_ref, out_ref
):
    rows, inner = x_ref.shape
    blocks = rows // SPAN
    causal, _ = tri_parts()
    lower = causal.astype(f32)
    acc, sig = conv_act(bc_ref[...].astype(f32), wb_ref[...], bb_ref[...])
    bc = (acc * sig).astype(bf16)
    b_blk = [bc[c * SPAN : (c + 1) * SPAN, :N] for c in range(blocks)]
    c_blk = [bc[c * SPAN : (c + 1) * SPAN, N:] for c in range(blocks)]
    cross = [dot(c_blk[c], b_blk[c], ((1,), (1,))) for c in range(blocks)]
    rated = [rates(c, step_ref, turn_ref, alog_ref, alog_turn_ref, lower) for c in range(blocks)]
    width = 2 * hsize
    lane = lax.broadcasted_iota(jnp.int32, (1, width), 1)
    masks = [(lane < hsize).astype(f32), (lane >= hsize).astype(f32)]
    for g in range(inner // width):
        cols = slice(g * width, (g + 1) * width)
        acc, sig = conv_act(x_ref[:, cols].astype(f32), wx_ref[:, cols], bx_ref[:, cols])
        vals = acc * sig
        state = None
        for c in range(blocks):
            span = slice(c * SPAN, (c + 1) * SPAN)
            _, within, within_turn = rated[c]
            v = vals[span]
            mix, split = [], []
            for i in range(2):
                h = 2 * g + i
                gap = within[:, h : h + 1] - within_turn[h : h + 1, :]
                mix.append(
                    (jnp.exp(jnp.where(causal, gap, -10000.0)) * cross[c] * turn_ref[h : h + 1, span]).astype(bf16)
                )
                split.append((v * masks[i]).astype(bf16))
            out = dot(jnp.concatenate(mix, axis=1), jnp.concatenate(split, axis=0))
            w0, w1 = within[:, 2 * g : 2 * g + 1], within[:, 2 * g + 1 : 2 * g + 2]
            if state is not None:
                out = out + lanes_of(hsize, jnp.exp(w0), jnp.exp(w1)) * dot(c_blk[c], state.astype(bf16))
            out_ref[span, cols] = out + skip_ref[:, cols] * v
            if c < blocks - 1:
                e0, e1 = w0[SPAN - 1 :], w1[SPAN - 1 :]
                tail = lanes_of(
                    hsize,
                    jnp.exp(e0 - w0) * step_ref[span, 2 * g : 2 * g + 1],
                    jnp.exp(e1 - w1) * step_ref[span, 2 * g + 1 : 2 * g + 2],
                )
                fresh = dot(b_blk[c], (tail * v).astype(bf16), ((0,), (0,)))
                if state is not None:
                    fresh = fresh + lanes_of(hsize, jnp.exp(e0), jnp.exp(e1)) * state
                state = fresh


def ssd_backward_kernel(
    hsize, x_ref, bc_ref, wx_ref, bx_ref, wb_ref, bb_ref, step_ref, turn_ref, alog_ref, alog_turn_ref, skip_ref,
    slope_ref, dy_ref, dx_ref, dbc_ref, ddt_ref, dwx_ref, dbx_ref, dwb_ref, dbb_ref, dhead_ref, dskip_ref,
    dcross_ref, dbmat_ref, dcmat_ref, col_ref, scol_ref, row_ref, srow_ref,
):
    rows, inner = x_ref.shape
    heads = step_ref.shape[1]
    blocks = rows // SPAN
    causal, eye = tri_parts()
    lower = causal.astype(f32)
    eye = eye.astype(f32)
    bc_in = bc_ref[...].astype(f32)
    bc_acc, bc_sig = conv_act(bc_in, wb_ref[...], bb_ref[...])
    bc = (bc_acc * bc_sig).astype(bf16)
    b_blk = [bc[c * SPAN : (c + 1) * SPAN, :N] for c in range(blocks)]
    c_blk = [bc[c * SPAN : (c + 1) * SPAN, N:] for c in range(blocks)]
    cross = [dot(c_blk[c], b_blk[c], ((1,), (1,))) for c in range(blocks)]
    rated = [rates(c, step_ref, turn_ref, alog_ref, alog_turn_ref, lower) for c in range(blocks)]
    for ref in (dcross_ref, dbmat_ref, dcmat_ref, col_ref, scol_ref, row_ref, srow_ref):
        ref[...] = jnp.zeros_like(ref)
    width = 2 * hsize
    lane = lax.broadcasted_iota(jnp.int32, (1, width), 1)
    masks = [(lane < hsize).astype(f32), (lane >= hsize).astype(f32)]
    head_lane = lax.broadcasted_iota(jnp.int32, (1, heads), 1)
    head_row = lax.broadcasted_iota(jnp.int32, (heads, 1), 0)
    last_row = lax.broadcasted_iota(jnp.int32, (SPAN, 1), 0) == SPAN - 1
    for g in range(inner // width):
        cols = slice(g * width, (g + 1) * width)
        x = x_ref[:, cols].astype(f32)
        acc, sig = conv_act(x, wx_ref[:, cols], bx_ref[:, cols])
        vals = acc * sig
        states, tails, decays = [None], [], []
        for c in range(blocks):
            span = slice(c * SPAN, (c + 1) * SPAN)
            within = rated[c][1]
            w0, w1 = within[:, 2 * g : 2 * g + 1], within[:, 2 * g + 1 : 2 * g + 2]
            e0, e1 = w0[SPAN - 1 :], w1[SPAN - 1 :]
            if c < blocks - 1:
                tails.append(
                    lanes_of(
                        hsize,
                        jnp.exp(e0 - w0) * step_ref[span, 2 * g : 2 * g + 1],
                        jnp.exp(e1 - w1) * step_ref[span, 2 * g + 1 : 2 * g + 2],
                    )
                )
                decays.append(lanes_of(hsize, jnp.exp(e0), jnp.exp(e1)))
                fresh = dot(b_blk[c], (tails[c] * vals[span]).astype(bf16), ((0,), (0,)))
                if states[c] is not None:
                    fresh = fresh + decays[c] * states[c]
                states.append(fresh)
        d_state = None
        d_vals = [None] * blocks
        d_skip = jnp.zeros((1, width), f32)
        for c in reversed(range(blocks)):
            span = slice(c * SPAN, (c + 1) * SPAN)
            _, within, within_turn = rated[c]
            v = vals[span]
            v_low = v.astype(bf16)
            dy = dy_ref[span, cols].astype(f32)
            ws = [within[:, 2 * g + i : 2 * g + i + 1] for i in range(2)]
            mix, split, d_w = [], [], []
            d_cross = None
            for i in range(2):
                h = 2 * g + i
                turn = turn_ref[h : h + 1, span]
                decay = jnp.exp(jnp.where(causal, ws[i] - within_turn[h : h + 1, :], -10000.0))
                scored = decay * cross[c]
                mix.append((scored * turn).astype(bf16))
                d_half = (dy * masks[i]).astype(bf16)
                split.append(d_half)
                d_mix = dot(d_half, v_low, ((1,), (1,)))
                raw = d_mix * scored
                part = d_mix * decay * turn
                d_cross = part if d_cross is None else d_cross + part
                d_w.append(jnp.sum(raw * turn, axis=1, keepdims=True))
                raw_sum = jnp.sum(raw, axis=0, keepdims=True)
                row_ref[c] += jnp.where(head_row == h, -raw_sum * turn, 0.0)
                srow_ref[c] += jnp.where(head_row == h, raw_sum, 0.0)
            dcross_ref[c] += d_cross
            d_v = dot(jnp.concatenate(mix, axis=0), jnp.concatenate(split, axis=0), ((0,), (0,)))
            d_v = d_v + skip_ref[:, cols] * dy
            d_skip = d_skip + jnp.sum(dy * v, axis=0, keepdims=True)
            d_enter = None
            if states[c] is not None:
                st = states[c].astype(bf16)
                lifted = lanes_of(hsize, jnp.exp(ws[0]), jnp.exp(ws[1])) * dy
                lift_low = lifted.astype(bf16)
                dcmat_ref[span] += dot(lift_low, st, ((1,), (1,)))
                d_enter = dot(c_blk[c], lift_low, ((0,), (0,)))
                prod = lifted * dot(c_blk[c], st)
                for i in range(2):
                    d_w[i] = d_w[i] + jnp.sum(prod * masks[i], axis=1, keepdims=True)
            if d_state is not None:
                ds_low = d_state.astype(bf16)
                back = dot(b_blk[c], ds_low)
                d_v = d_v + tails[c] * back
                dbmat_ref[span] += dot((tails[c] * v).astype(bf16), ds_low, ((1,), (1,)))
                along = v * back
                if states[c] is not None:
                    held = decays[c] * d_state * states[c]
                for i in range(2):
                    h = 2 * g + i
                    d_tail = jnp.sum(along * masks[i], axis=1, keepdims=True)
                    reach = jnp.exp(ws[i][SPAN - 1 :] - ws[i])
                    scol_ref[c] += jnp.where(head_lane == h, d_tail * reach, 0.0)
                    fall = d_tail * reach * step_ref[span, h : h + 1]
                    d_end = jnp.sum(fall, axis=0, keepdims=True)
                    if states[c] is not None:
                        d_end = d_end + jnp.sum(
                            jnp.sum(held * masks[i], axis=1, keepdims=True), axis=0, keepdims=True
                        )
                    d_w[i] = d_w[i] - fall + jnp.where(last_row, d_end, 0.0)
                if d_enter is not None:
                    d_enter = d_enter + decays[c] * d_state
            for i in range(2):
                col_ref[c] += jnp.where(head_lane == 2 * g + i, d_w[i], 0.0)
            d_state = d_enter
            d_vals[c] = d_v
        d_acc = jnp.concatenate(d_vals, axis=0) * (sig + vals * (1.0 - sig))
        d_x, d_taps, d_bias = conv_back(x, wx_ref[:, cols], d_acc)
        dx_ref[:, cols] = d_x.astype(bf16)
        for k in range(K):
            dwx_ref[k : k + 1, cols] = d_taps[k]
        dbx_ref[:, cols] = d_bias
        dskip_ref[:, cols] = d_skip
    d_alog = jnp.zeros((1, heads), f32)
    d_dtb = jnp.zeros((1, heads), f32)
    for c in range(blocks):
        span = slice(c * SPAN, (c + 1) * SPAN)
        d_w = col_ref[c] + fine(eye, row_ref[c], ((1,), (1,)))
        d_step = scol_ref[c] + fine(eye, srow_ref[c], ((1,), (1,)))
        d_rate = fine(lower, d_w, ((0,), (0,)))
        d_alog = d_alog + jnp.sum(rated[c][0] * d_rate, axis=0, keepdims=True)
        d_dt = (d_step - jnp.exp(alog_ref[...]) * d_rate) * slope_ref[span, :]
        ddt_ref[span, :] = d_dt
        d_dtb = d_dtb + jnp.sum(d_dt, axis=0, keepdims=True)
        low = dcross_ref[c].astype(bf16)
        dcmat_ref[span] += dot(low, b_blk[c])
        dbmat_ref[span] += dot(low, c_blk[c], ((0,), (0,)))
    dhead_ref[0:1, :] = d_alog
    dhead_ref[1:2, :] = d_dtb
    d_bc = jnp.concatenate([dbmat_ref[...], dcmat_ref[...]], axis=1)
    d_acc = d_bc * (bc_sig + bc_acc * bc_sig * (1.0 - bc_sig))
    d_x, d_taps, d_bias = conv_back(bc_in, wb_ref[...], d_acc)
    dbc_ref[...] = d_x
    for k in range(K):
        dwb_ref[k : k + 1, :] = d_taps[k]
    dbb_ref[...] = d_bias


def vmem_specs(count):
    return [pl.BlockSpec(memory_space=pltpu.VMEM)] * count


def ssd_forward(hsize, args):
    return pl.pallas_call(
        functools.partial(ssd_forward_kernel, hsize),
        out_shape=jax.ShapeDtypeStruct(args[0].shape, f32),
        in_specs=vmem_specs(len(args)),
        out_specs=vmem_specs(1)[0],
        cost_estimate=pl.CostEstimate(flops=int(2.5e9), transcendentals=0, bytes_accessed=int(1e7)),
        name="ssd_forward",
    )(*args)


def ssd_backward(hsize, args):
    rows, inner = args[0].shape
    heads = args[6].shape[1]
    blocks = rows // SPAN
    shapes = [
        ((rows, inner), bf16),
        ((rows, 2 * N), f32),
        ((rows, heads), f32),
        ((K, inner), f32),
        ((1, inner), f32),
        ((K, 2 * N), f32),
        ((1, 2 * N), f32),
        ((2, heads), f32),
        ((1, inner), f32),
    ]
    return pl.pallas_call(
        functools.partial(ssd_backward_kernel, hsize),
        out_shape=[jax.ShapeDtypeStruct(a, b) for a, b in shapes],
        in_specs=vmem_specs(len(args)),
        out_specs=vmem_specs(len(shapes)),
        scratch_shapes=[
            pltpu.VMEM((blocks, SPAN, SPAN), f32),
            pltpu.VMEM((rows, N), f32),
            pltpu.VMEM((rows, N), f32),
            pltpu.VMEM((blocks, SPAN, heads), f32),
            pltpu.VMEM((blocks, SPAN, heads), f32),
            pltpu.VMEM((blocks, heads, SPAN), f32),
            pltpu.VMEM((blocks, heads, SPAN), f32),
        ],
        cost_estimate=pl.CostEstimate(flops=int(6e9), transcendentals=0, bytes_accessed=int(2.4e7)),
        name="ssd_backward",
    )(*args)


def adamw(param_vec, grad_vec, first, second):
    first_new = beta_one * first + (1.0 - beta_one) * grad_vec
    second_new = beta_two * second + (1.0 - beta_two) * grad_vec * grad_vec
    first_hat = first_new / (1.0 - beta_one**adam_step)
    second_hat = second_new / (1.0 - beta_two**adam_step)
    updated = param_vec - learn_rate * (
        first_hat / (jnp.sqrt(second_hat) + adam_eps) + weight_decay * param_vec
    )
    return (updated, first_new, second_new)


class Plan:
    def __init__(self, dp, seq, flat):
        self.dp, self.seq, self.flat = dp, seq, flat
        self.total = dp * seq
        count = self.total
        self.mix = IN // flat
        last_in = -(-IN // flat)
        rows_in = max(
            -(-(((k * flat) % PROJ) + min(flat, IN - k * flat)) // PROJ) for k in range(last_in)
        )
        rows_out = max(
            -(-(((k * flat - IN) % D) + flat) // D) for k in range(self.mix, count)
        )
        self.rows = ceil_to(max(rows_in, -(-rows_out // 4)), 8)
        self.in_len = IN - self.mix * flat
        self.mix_in = -(-(((self.mix * flat) % PROJ) + self.in_len) // PROJ)
        self.mix_out = -(-(flat - self.in_len) // D)
        self.mix_free = self.rows - self.mix_in
        assert 4 * self.mix_free >= self.mix_out
        rows = self.rows
        self.j_in = self.mix // seq + 1
        self.j_out = self.mix // seq
        n_in, n_out = self.j_in, dp - self.j_out
        self.in_map = np.full((seq, n_in, rows), -1, np.int32)
        self.out_map = np.full((seq, n_out, 4, rows), -1, np.int32)
        m = np.arange(rows)
        for s in range(seq):
            for j in range(n_in):
                k = j * seq + s
                if k > self.mix:
                    continue
                first = (k * flat) // PROJ
                used = min(rows, D - first)
                if k == self.mix:
                    used = self.mix_in
                self.in_map[s, j, :used] = first + m[:used]
            for j in range(n_out):
                k = (j + self.j_out) * seq + s
                if k < self.mix:
                    continue
                for b in range(4):
                    if k == self.mix:
                        q = b * self.mix_free + (m - self.mix_in)
                        ok = (m >= self.mix_in) & (q < self.mix_out)
                    else:
                        q = (k * flat - IN) // D + b * rows + m
                        ok = q < min(DI, -(-((k + 1) * flat - IN) // D))
                    self.out_map[s, j, b] = np.where(ok, q, -1)

    def windows(self):
        rows, seq = self.rows, self.seq
        table = np.zeros((seq, self.dp - self.j_out, 4, 3), np.int32)
        for s in range(seq):
            for j in range(self.dp - self.j_out):
                k = (j + self.j_out) * seq + s
                for b in range(4):
                    if k < self.mix:
                        continue
                    if k == self.mix:
                        start = b * self.mix_free - self.mix_in
                        low = self.mix_in
                        high = min(rows, low + max(0, self.mix_out - b * self.mix_free))
                    else:
                        start = (k * self.flat - IN) // D + b * rows
                        low = 0
                        stop = min(DI, -(-((k + 1) * self.flat - IN) // D))
                        high = min(rows, max(0, stop - start))
                    table[s, j, b] = ((start + s * (DI // seq)) % DI, low, high)
        return table.reshape(seq, -1)

    def pack(self, flat, k):
        rows, size = self.rows, self.flat
        shift = (k * size) % PROJ
        span = rows * PROJ
        buf = jnp.pad(flat, (PROJ, span - size))
        win = lax.dynamic_slice(buf, (PROJ - shift,), (span,)).reshape(rows, PROJ)
        win = jnp.pad(win, ((0, 0), (0, WIDE - PROJ)))
        off = (k * size - IN) % D
        span = 4 * rows * D
        buf = jnp.pad(flat, (D, span - size))
        out = lax.dynamic_slice(buf, (D - off,), (span,)).reshape(4, rows, D)
        out = jnp.concatenate([out[b] for b in range(4)] + [jnp.zeros((rows, WIDE - 4 * D), flat.dtype)], axis=1)
        head = flat[self.in_len :]
        free = self.mix_free
        head = jnp.pad(head, (0, 4 * free * D - head.shape[0])).reshape(4, free, D)
        low = jnp.concatenate([head[b] for b in range(4)] + [jnp.zeros((free, WIDE - 4 * D), flat.dtype)], axis=1)
        mixed = jnp.concatenate([win[: self.mix_in], low], axis=0)
        return jnp.where(k < self.mix, win, jnp.where(k > self.mix, out, mixed))

    def unpack(self, chunk, k):
        rows, size = self.rows, self.flat
        shift = (k * size) % PROJ
        line = chunk[:, :PROJ].reshape(-1)
        line = jnp.pad(line, (0, max(0, PROJ + size - rows * PROJ)))
        win = lax.dynamic_slice(line, (shift,), (size,))
        off = (k * size - IN) % D
        line = jnp.concatenate([chunk[:, b * D : (b + 1) * D] for b in range(4)], axis=0).reshape(-1)
        line = jnp.pad(line, (0, max(0, D + size - 4 * rows * D)))
        out = lax.dynamic_slice(line, (off,), (size,))
        low = chunk[self.mix_in :]
        low = jnp.concatenate([low[:, b * D : (b + 1) * D] for b in range(4)], axis=0)
        mixed = jnp.concatenate([win[: self.in_len], low.reshape(-1)[: size - self.in_len]])
        return jnp.where(k < self.mix, win, jnp.where(k > self.mix, out, mixed))


def make_general(dp, seq):
    za, yb, cc = factors(dp)

    def place(z, y, c):
        return ((z % za) * yb + (y % yb)) * cc + (c % cc)

    def perm(dz, dy, dc):
        return [
            (place(z, y, c), place(z + dz, y + dy, c + dc))
            for z in range(za)
            for y in range(yb)
            for c in range(cc)
        ]

    z_next, y_next, c_next = perm(1, 0, 0), perm(0, 1, 0), perm(0, 0, 1)

    def gather_dp(chunk):
        j = lax.axis_index("dp")
        z, y, c = j // (yb * cc), (j // cc) % yb, j % cc
        whole = jnp.zeros((dp,) + chunk.shape, chunk.dtype)
        slots = []
        cur = chunk
        for r in range(za):
            if r:
                cur = lax.ppermute(cur, "dp", z_next)
            side = cur
            for t in range(yb):
                if t:
                    side = lax.ppermute(side, "dp", y_next)
                slots.append((z - r, y - t, c, side))
                if cc == 2:
                    slots.append((z - r, y - t, c + 1, lax.ppermute(side, "dp", c_next)))
        for zi, yi, ci, data in slots:
            at = (((zi + za) % za) * yb + (yi + yb) % yb) * cc + ci % cc
            whole = lax.dynamic_update_index_in_dim(whole, data, at, 0)
        return whole

    def scatter_dp(parts):
        j = lax.axis_index("dp")
        z, y, c = j // (yb * cc), (j // cc) % yb, j % cc

        def pick(zi, yi, ci):
            at = (((zi + za) % za) * yb + (yi + yb) % yb) * cc + ci % cc
            return lax.dynamic_index_in_dim(parts, at, 0, False)

        def core_sum(zi, yi):
            own = pick(zi, yi, c)
            if cc == 2:
                got = lax.ppermute(pick(zi, yi, c + 1), "dp", c_next)
                own = (own.astype(f32) + got.astype(f32)).astype(bf16)
            return own

        def mid_sum(zi):
            acc = None
            for r in range(1, yb + 1):
                mine = core_sum(zi, y - r)
                if acc is not None:
                    acc = (acc.astype(f32) + mine.astype(f32)).astype(bf16)
                else:
                    acc = mine
                if r < yb:
                    acc = lax.ppermute(acc, "dp", y_next)
            return acc

        acc = None
        for r in range(1, za + 1):
            mine = mid_sum(z - r)
            if acc is not None:
                acc = acc.astype(f32) + mine.astype(f32)
            else:
                acc = mine
            if r < za:
                acc = lax.ppermute(acc.astype(bf16), "dp", z_next)
        return acc.astype(f32)

    def swap_seq(a):
        return lax.ppermute(a, "seq", [(0, 1), (1, 0)])

    def halves(a, axis):
        n = a.shape[axis] // 2
        return lax.slice_in_dim(a, 0, n, axis=axis), lax.slice_in_dim(a, n, 2 * n, axis=axis)

    def gather_seq(a, axis):
        if seq != 2:
            return lax.all_gather(a, "seq", axis=axis, tiled=True)
        first = lax.axis_index("seq") == 0
        other = swap_seq(a)
        return jnp.concatenate([jnp.where(first, a, other), jnp.where(first, other, a)], axis=axis)

    def scatter_seq(a, axis):
        if seq != 2:
            return lax.psum_scatter(a, "seq", scatter_dimension=axis, tiled=True)
        first = lax.axis_index("seq") == 0
        low, high = halves(a, axis)
        got = swap_seq(jnp.where(first, high, low).astype(bf16))
        return jnp.where(first, low, high) + got.astype(f32)

    def sum_seq(a):
        if seq != 2:
            return lax.psum(a, "seq")
        a = a.astype(bf16)
        return a.astype(f32) + swap_seq(a).astype(f32)

    def sum_seq_wide(a):
        if seq != 2:
            return lax.psum(a, "seq")
        return a + swap_seq(a)

    def own_seq(a, axis):
        n = a.shape[axis] // seq
        return lax.dynamic_slice_in_dim(a, lax.axis_index("seq") * n, n, axis)

    def sum_all(a):
        for axis, count in (("seq", seq), ("dp", dp)):
            step = 1
            while step < count:
                a = a + lax.ppermute(a, axis, [(i, i ^ step) for i in range(count)])
                step *= 2
        return a

    def on_device(x_in, cotangent, params, moment_one, moment_two):
        size = params.shape[0]
        plan = Plan(dp, seq, size)
        rows = plan.rows
        s = lax.axis_index("seq")
        k = lax.axis_index("dp") * seq + s
        halfs = params.astype(bf16)

        x_own = x_in[0]
        cot_own = cotangent[0]
        tokens = gather_seq(x_own, 0)
        cot = gather_seq(cot_own, 0)

        base = IN + OUT
        at = base - k * size
        padded = jnp.pad(halfs, (SMALL, SMALL))
        tail = lax.dynamic_slice(padded, (jnp.clip(at + SMALL, 0, size + SMALL),), (SMALL,))
        tail = jnp.pad(tail, (0, -SMALL % D)).reshape(-1, D)
        small = sum_all(tail).reshape(-1)
        pieces = []
        offset = 0
        for length in (K * CONV, CONV, D, DI, H, H, H):
            pieces.append(small[offset : offset + length].astype(f32))
            offset += length
        conv_w, conv_b, norm_g, gate_g, a_log, dt_bias, skip_gain = pieces
        conv_w = conv_w.reshape(K, CONV)

        chunk = plan.pack(halfs, k)
        whole = gather_dp(chunk)
        n_in, n_out = plan.j_in, dp - plan.j_out
        w_in = whole[:n_in].reshape(n_in * rows, WIDE)
        w_out = [
            whole[plan.j_out :, :, b * D : (b + 1) * D].reshape(n_out * rows, D) for b in range(4)
        ]
        in_map = lax.dynamic_index_in_dim(jnp.asarray(plan.in_map.reshape(seq, -1)), s, 0, False)
        out_map = lax.dynamic_index_in_dim(
            jnp.asarray(plan.out_map.transpose(0, 2, 1, 3).reshape(seq, 4, -1)), s, 0, False
        )
        pick_in = (jnp.arange(D)[:, None] == in_map[None, :]).astype(bf16)
        pick_out = [(jnp.arange(DI)[:, None] == out_map[b][None, :]).astype(bf16) for b in range(4)]

        wide = tokens.astype(f32)
        scale = lax.rsqrt(jnp.mean(wide * wide, axis=-1, keepdims=True) + norm_eps)
        normed = (wide * scale * norm_g[None, :]).astype(bf16)
        normed_k = dot(normed, pick_in).astype(bf16)
        partial = dot(normed_k, w_in)

        x_part = scatter_seq(partial[:, DI : 2 * DI], 1)
        bcdt = sum_seq(partial[:, 2 * DI : PROJ])
        z_part = scatter_seq(partial[:, :DI], 1)
        gate_in = z_part.astype(bf16).astype(f32)
        x_pre = x_part.astype(bf16)
        bc_pre = bcdt[:, : 2 * N].astype(bf16)
        dt_raw = own_seq(bcdt[:, 2 * N :], 1).astype(bf16).astype(f32)
        hsize = DI // H
        dt_in = dt_raw + own_seq(dt_bias, 0)[None, :]
        step_size = jax.nn.softplus(dt_in)
        alog = own_seq(a_log, 0)[None, :]
        ssd_args = (
            x_pre,
            bc_pre,
            own_seq(conv_w[:, :DI], 1),
            own_seq(conv_b[:DI], 0)[None, :],
            conv_w[:, DI:],
            conv_b[None, DI:],
            step_size,
            step_size.T,
            alog,
            alog.T,
            jnp.repeat(own_seq(skip_gain, 0), hsize)[None, :],
        )
        ssd_out = ssd_forward(hsize, ssd_args)

        d_gated = None
        for b in range(4):
            piece = dot(cot, w_out[b], ((1,), (1,))).astype(bf16)
            piece = dot(piece, pick_out[b], ((1,), (1,)))
            d_gated = piece if d_gated is None else d_gated + piece
        d_gated = scatter_seq(d_gated, 1)

        gain = own_seq(gate_g, 0)[None, :]
        sig = jax.nn.sigmoid(gate_in)
        swish = gate_in * sig
        gated = ssd_out * swish
        weighted = d_gated * gain
        sums = jnp.stack([jnp.sum(gated * gated, axis=1), jnp.sum(weighted * gated, axis=1)])
        sums = sum_seq_wide(sums)
        g_scale = lax.rsqrt(sums[0] / DI + norm_eps)[:, None]
        cross = (sums[1] / DI)[:, None]
        gated_norm = (gated * g_scale * gain).astype(bf16)
        d_gate_g = jnp.sum(d_gated * gated * g_scale, axis=0)
        d_pre = g_scale * weighted - gated * g_scale**3 * cross
        d_ssd = d_pre * swish
        d_gate_in = d_pre * ssd_out * (sig + swish * (1.0 - sig))

        gn_full = gather_seq(gated_norm, 1)
        gn_k = [dot(gn_full, pick_out[b]).astype(bf16) for b in range(4)]
        y_part = None
        for b in range(4):
            piece = dot(gn_k[b], w_out[b])
            y_part = piece if y_part is None else y_part + piece
        y_own = scatter_seq(y_part, 0) + x_own.astype(f32)

        d_x, d_bcpre, d_dtraw, d_wx, d_bx, d_wb, d_bb, d_head, d_skip = ssd_backward(
            hsize, ssd_args + (jax.nn.sigmoid(dt_in), d_ssd)
        )
        d_alog, d_dtbias = d_head[0], d_head[1]
        d_skip = jnp.sum(d_skip.reshape(-1, hsize), axis=1)
        d_z_full = gather_seq(d_gate_in.astype(bf16), 1)
        d_x_full = gather_seq(d_x, 1)
        d_bc = sum_seq(d_bcpre).astype(bf16)
        d_dt_full = gather_seq(d_dtraw.astype(bf16), 1)
        pad = jnp.zeros((d_bc.shape[0], WIDE - PROJ), bf16)
        d_mixed = jnp.concatenate([d_z_full, d_x_full, d_bc, d_dt_full, pad], axis=1)

        g_in = dot(normed_k, d_mixed, ((0,), (0,))).astype(bf16).reshape(n_in, rows, WIDE)
        g_out = jnp.concatenate(
            [dot(gn_k[b], cot, ((0,), (0,))).astype(bf16).reshape(n_out, rows, D) for b in range(4)]
            + [jnp.zeros((n_out, rows, WIDE - 4 * D), bf16)],
            axis=2,
        )
        both = n_in + n_out - dp
        parts = jnp.concatenate(
            [g_in[: n_in - both], g_in[n_in - both :] + g_out[:both], g_out[both:]], axis=0
        )

        dn_k = dot(d_mixed, w_in, ((1,), (1,))).astype(bf16)
        d_normed = scatter_seq(dot(dn_k, pick_in, ((1,), (1,))), 0)
        wide_own = x_own.astype(f32)
        scale_own = lax.rsqrt(jnp.mean(wide_own * wide_own, axis=-1, keepdims=True) + norm_eps)
        a_own = d_normed * norm_g[None, :]
        d_norm_g = jnp.sum(d_normed * wide_own * scale_own, axis=0)
        d_wide = scale_own * a_own - wide_own * scale_own**3 * jnp.mean(
            a_own * wide_own, axis=-1, keepdims=True
        )
        input_grad = (cot_own.astype(f32) + d_wide).astype(bf16)

        def spread(a, width):
            full = jnp.zeros(a.shape[:-1] + (width,), f32)
            start = (0,) * (a.ndim - 1) + (s * a.shape[-1],)
            return lax.dynamic_update_slice(full, a, start)

        small_grad = jnp.concatenate(
            [
                jnp.concatenate([spread(d_wx, DI), d_wb], axis=1).reshape(-1),
                spread(d_bx[0], DI),
                d_bb[0],
                d_norm_g,
                spread(d_gate_g, DI),
                spread(d_alog, H),
                spread(d_dtbias, H),
                spread(d_skip, H),
            ]
        )
        small_grad = jnp.pad(small_grad, (0, -SMALL % D)).reshape(-1, D)
        small_grad = sum_all(small_grad).reshape(-1)[:SMALL]

        grad_chunk = scatter_dp(parts)
        shard = plan.unpack(grad_chunk, k)
        wing = jnp.pad(small_grad, (size, size))
        shard = shard + lax.dynamic_slice(
            wing, (jnp.clip(size - at, 0, size + SMALL),), (size,)
        )
        updated, first_new, second_new = adamw(params, shard, moment_one, moment_two)
        return (y_own.astype(bf16)[None], input_grad[None], shard, updated, first_new, second_new)

    return on_device


def matmul_cost(flops, size):
    return pl.CostEstimate(flops=flops, transcendentals=0, bytes_accessed=size)


def call(kernel, shapes, args, micros, scratch=(), tables=0, raw=0):
    specs = [pl.BlockSpec(memory_space=pltpu.SMEM)] * tables
    specs += [pl.BlockSpec(memory_space=pl.ANY)] * raw
    specs += vmem_specs(len(args) - tables - raw)
    return pl.pallas_call(
        kernel,
        out_shape=[jax.ShapeDtypeStruct(a, b) for a, b in shapes],
        in_specs=specs,
        out_specs=vmem_specs(len(shapes)),
        scratch_shapes=list(scratch),
        cost_estimate=matmul_cost(int(micros * 5e8), int(micros * 2e6)),
    )(*args)


def front_kernel(depth, slots, rows, at_ref, *refs):
    parts, nk_ref, w_ref, own_ref, other_ref = refs[:slots], *refs[slots : slots + 4]
    sems = refs[-1]
    copies = []
    for i, part in enumerate(parts):
        start = pl.multiple_of(at_ref[i] * rows, 8)
        copies.append(pltpu.make_async_copy(part, w_ref.at[pl.ds(start, rows), :], sems.at[i]))
    for copy in copies:
        copy.start()
    for copy in copies:
        copy.wait()
    half = own_ref.shape[1]
    nk = nk_ref[...]
    own_ref[...] = dot(nk, w_ref[:depth, :half])
    other_ref[...] = dot(nk, w_ref[:depth, half : 2 * half]).astype(bf16)
    if len(refs) > slots + 5:
        refs[slots + 4][...] = dot(nk, w_ref[:depth, 2 * half :]).astype(bf16)


def window_mask(rows, low, high):
    at = lax.broadcasted_iota(jnp.int32, (rows, 1), 0)
    return (at >= low) & (at < high)


def gate_grad_kernel(base, rows, tab_ref, wb_ref, wa_ref, cot_ref, own_ref, other_ref, buf_ref, acc_ref, sems):
    half = own_ref.shape[1]
    count = buf_ref.shape[1]
    copies = []
    for b in range(4):
        ref = wb_ref if b < 2 else wa_ref
        c = b % 2
        copies.append(
            pltpu.make_async_copy(
                ref.at[pl.ds(base, count), pl.ds(c * D, D)], buf_ref.at[b], sems.at[b]
            )
        )
    for copy in copies:
        copy.start()
    acc_ref[...] = jnp.zeros_like(acc_ref)
    for b in range(4):
        copies[b].wait()
        piece = dot(buf_ref[b], cot_ref[...], ((1,), (1,)))
        for j in range(count // rows):
            n = (j * 4 + b) * 3
            keep = window_mask(rows, tab_ref[n + 1], tab_ref[n + 2])
            part = jnp.where(keep, piece[j * rows : (j + 1) * rows], 0.0)
            part = jnp.concatenate([part, jnp.zeros((8, part.shape[1]), f32)], axis=0)
            start = tab_ref[n]
            near = pl.multiple_of((start // 8) * 8, 8)
            acc_ref[pl.ds(near, rows + 8), :] += pltpu.roll(part, start - near, 0)
    acc_ref[: rows + 8] += acc_ref[DI : DI + rows + 8]
    own_ref[...] = acc_ref[:half].T
    other_ref[...] = acc_ref[half : 2 * half].T.astype(bf16)


def pick_kernel(rows, tab_ref, own_ref, other_ref, gk_ref, turn_ref):
    half = own_ref.shape[1]
    turn_ref[:half] = own_ref[...].astype(f32).T
    turn_ref[half : 2 * half] = other_ref[...].astype(f32).T
    turn_ref[DI : DI + rows + 8] = turn_ref[: rows + 8]
    for b in range(4):
        for j in range(gk_ref.shape[1] // rows):
            n = (j * 4 + b) * 3
            keep = window_mask(rows, tab_ref[n + 1], tab_ref[n + 2])
            start = tab_ref[n]
            near = pl.multiple_of((start // 8) * 8, 8)
            part = pltpu.roll(turn_ref[pl.ds(near, rows + 8), :], (rows + 8 - (start - near)) % (rows + 8), 0)
            part = jnp.where(keep, part[:rows], 0.0)
            gk_ref[b, j * rows : (j + 1) * rows, :] = part.astype(bf16)


def out_kernel(base, wb_ref, wa_ref, gk_ref, y_ref, buf_ref, sems):
    count = buf_ref.shape[1]
    copies = []
    for b in range(4):
        ref = wb_ref if b < 2 else wa_ref
        c = b % 2
        copies.append(
            pltpu.make_async_copy(
                ref.at[pl.ds(base, count), pl.ds(c * D, D)], buf_ref.at[b], sems.at[b]
            )
        )
    for copy in copies:
        copy.start()
    total = None
    for b in range(4):
        copies[b].wait()
        piece = dot(gk_ref[b], buf_ref[b], ((0,), (0,)))
        total = piece if total is None else total + piece
    y_ref[...] = total


def weight_grad_kernel(depth, base, first, nk_ref, d_ref, gk_ref, cot_ref, out_ref):
    cols = out_ref.shape[1]
    nk = nk_ref[...]
    for n in range(0, cols, D):
        stop = min(n + D, cols)
        top = dot(nk, d_ref[:, n:stop], ((0,), (0,)))
        out_ref[:base, n:stop] = top[:base].astype(bf16)
        if n + D <= 2 * D:
            low = dot(gk_ref[first + n // D], cot_ref[...])
            out_ref[base:depth, n:stop] = (top[base:] + low[: depth - base]).astype(bf16)
            out_ref[depth:, n:stop] = low[depth - base :].astype(bf16)
        else:
            out_ref[base:depth, n:stop] = top[base:].astype(bf16)
            out_ref[depth:, n:stop] = jnp.zeros((out_ref.shape[0] - depth, stop - n), bf16)


def input_grad_kernel(depth, db_ref, da_ref, wb_ref, wa_ref, pick_ref, out_ref):
    dn = dot(db_ref[...], wb_ref[:depth], ((1,), (1,))) + dot(da_ref[...], wa_ref[:depth], ((1,), (1,)))
    out_ref[...] = dot(dn.astype(bf16), pick_ref[...], ((1,), (1,)))


def tie(value, token):
    return lax.optimization_barrier((value, token))[0]


def small_fits(dp, plan):
    start = (dp - 1) * plan.seq
    return plan.rows * (WIDE - 4 * D) >= SMALL and start > plan.mix and start * plan.flat <= IN + OUT


def make_pair(dp, flat):
    seq = 2
    plan = Plan(dp, seq, flat)
    rows = plan.rows
    za, yb, cc = factors(dp)
    inner = DI // seq
    hsize = DI // H
    side = WIDE - 4 * D
    n_in, n_out = plan.j_in, dp - plan.j_out
    depth, base = n_in * rows, plan.j_out * rows

    def place(z, y, c):
        return ((z % za) * yb + (y % yb)) * cc + (c % cc)

    def perm(dz, dy, dc):
        return [
            (place(z, y, c), place(z + dz, y + dy, c + dc))
            for z in range(za)
            for y in range(yb)
            for c in range(cc)
        ]

    z_next, y_next, c_next = perm(1, 0, 0), perm(0, 1, 0), perm(0, 0, 1)

    def position():
        j = lax.axis_index("dp")
        return j // (yb * cc), (j // cc) % yb, j % cc

    def index(z, y, c):
        return (((z + za) % za) * yb + (y + yb) % yb) * cc + c % cc

    def gather_dp(chunk):
        z, y, c = position()
        slots = []
        marks = []
        cur = chunk
        for r in range(za):
            if r:
                cur = lax.ppermute(cur, "dp", z_next)
                marks.append(cur)
            beside = cur
            for t in range(yb):
                if t:
                    beside = lax.ppermute(beside, "dp", y_next)
                if cc == 2:
                    slots.append((index(z - r, y - t, c + 1), lax.ppermute(beside, "dp", c_next)))
                slots.append((index(z - r, y - t, c), beside))
        return jnp.stack([at for at, _ in slots]).astype(jnp.int32), [data for _, data in slots], marks

    def scatter_dp(parts):
        parts = parts.reshape(za, yb, cc, rows, -1)
        z, y, c = position()

        def add(a, b):
            return (a.astype(f32) + b.astype(f32)).astype(bf16)

        total = lax.dynamic_index_in_dim(parts, c, 2, False)
        if cc == 2:
            give = lax.dynamic_index_in_dim(parts, (c + 1) % cc, 2, False)
            give = lax.ppermute(give, "dp", c_next)
            total = add(total, give)
        total = total.reshape(za * yb, rows, -1)

        def core_sum(zi, yi):
            return lax.dynamic_index_in_dim(total, ((zi + za) % za) * yb + (yi + yb) % yb, 0, False)

        def mid_sum(zi):
            acc = core_sum(zi, y - 1)
            for r in range(2, yb + 1):
                acc = lax.ppermute(acc, "dp", y_next)
                acc = add(acc, core_sum(zi, y - r))
            return acc

        acc = mid_sum(z - 1)
        marks = [acc]
        for r in range(2, za + 1):
            acc = add(lax.ppermute(acc, "dp", z_next), mid_sum(z - r))
            marks.append(acc)
        return acc, marks

    def swap(a):
        return lax.ppermute(a, "seq", [(0, 1), (1, 0)])

    def sum_all(a, marks):
        a = a + swap(a)
        steps = []
        step = 1
        while step < dp:
            steps.append(step)
            step *= 2
        steps = steps[:1] + steps[2:] + steps[1:2]
        for n, step in enumerate(steps):
            got = lax.ppermute(a, "dp", [(i, i ^ step) for i in range(dp)])
            if n:
                got = tie(got, marks[min(n - 1, len(marks) - 1)])
            a = a + got
        return a

    def own_seq(a, axis):
        n = a.shape[axis] // seq
        return lax.dynamic_slice_in_dim(a, lax.axis_index("seq") * n, n, axis)

    def on_device(x_in, cotangent, params, moment_one, moment_two):
        s = lax.axis_index("seq")
        first = s == 0
        k = lax.axis_index("dp") * seq + s
        halfs = params.astype(bf16)

        def ordered(a, other):
            return jnp.concatenate([jnp.where(first, a, other), jnp.where(first, other, a)], axis=0)

        def flip(a, cut):
            return jnp.where(first, a, jnp.concatenate([a[:, cut:], a[:, :cut]], axis=1))

        at = IN + OUT - k * flat
        padded = jnp.pad(halfs, (SMALL, SMALL))
        tail = lax.dynamic_slice(padded, (jnp.clip(at + SMALL, 0, flat + SMALL),), (SMALL,))
        tail = jnp.pad(tail, (0, rows * side - SMALL)).reshape(rows, side)
        tail = tail + swap(tail)

        chunk = plan.pack(halfs, k)
        input_rows = k <= plan.mix
        part_b = jnp.where(input_rows, flip(chunk[:, :DI], inner), chunk[:, :DI])
        mid = chunk[:, DI : 2 * DI]
        part_a = jnp.concatenate(
            [
                jnp.where(input_rows, flip(mid, inner), mid),
                jnp.where(input_rows, chunk[:, 4 * D :], tail),
            ],
            axis=1,
        )
        if plan.mix_out:
            keep = (k == plan.mix) & (jnp.arange(rows) >= plan.mix_in)[:, None]
            part_b = jnp.where(keep, chunk[:, :DI], part_b)
            part_a = jnp.where(keep, chunk[:, DI:], part_a)
        at_a, slots_a, marks = gather_dp(part_a)
        part_b = tie(part_b, marks[-1])
        late = marks[1 % len(marks)]

        x_own = x_in[0]
        cot_own = cotangent[0]
        tokens = ordered(x_own, tie(swap(x_own), late))
        cot = ordered(cot_own, tie(swap(cot_own), late))
        count = tokens.shape[0]

        in_map = lax.dynamic_index_in_dim(jnp.asarray(plan.in_map.reshape(seq, -1)), tie(s, late), 0, False)
        table = lax.dynamic_index_in_dim(jnp.asarray(plan.windows()), s, 0, False)
        pick_in = (jnp.arange(D)[:, None] == in_map[None, :]).astype(bf16)
        mine = at_a == dp - 1
        small = functools.reduce(
            jnp.add, [jnp.where(mine[i], a[:, 2 * D :], 0) for i, a in enumerate(slots_a)]
        ).reshape(-1)
        pieces = []
        offset = 0
        for length in (K * CONV, CONV, D, DI, H, H, H):
            pieces.append(small[offset : offset + length].astype(f32))
            offset += length
        conv_w, conv_b, norm_g, gate_g, a_log, dt_bias, skip_gain = pieces
        conv_w = conv_w.reshape(K, CONV)

        wide = tokens.astype(f32)
        scale = lax.rsqrt(jnp.mean(wide * wide, axis=-1, keepdims=True) + norm_eps)
        normed = (wide * scale * norm_g[None, :]).astype(bf16)
        normed_k = dot(normed, pick_in).astype(bf16)

        w_a, x_own_part, x_other, bcdt = call(
            functools.partial(front_kernel, depth, dp, rows),
            [
                ((dp * rows, 2 * D + side), bf16),
                ((count, inner), f32),
                ((count, inner), bf16),
                ((count, side), bf16),
            ],
            (at_a, *slots_a, normed_k),
            5.0,
            scratch=[pltpu.SemaphoreType.DMA((dp,))],
            tables=1,
            raw=dp,
        )
        at_b, slots_b, marks = gather_dp(part_b)
        bcdt = bcdt.astype(f32) + tie(swap(bcdt), marks[-1]).astype(f32)
        x_pre = (x_own_part + swap(x_other).astype(f32)).astype(bf16)
        bc_pre = bcdt[:, : 2 * N].astype(bf16)
        dt_raw = own_seq(bcdt[:, 2 * N : 2 * N + H], 1).astype(bf16).astype(f32)
        dt_in = dt_raw + own_seq(dt_bias, 0)[None, :]
        step_size = jax.nn.softplus(dt_in)
        alog = own_seq(a_log, 0)[None, :]
        ssd_args = (
            x_pre,
            bc_pre,
            own_seq(conv_w[:, :DI], 1),
            own_seq(conv_b[:DI], 0)[None, :],
            conv_w[:, DI:],
            conv_b[None, DI:],
            step_size,
            step_size.T,
            alog,
            alog.T,
            jnp.repeat(own_seq(skip_gain, 0), hsize)[None, :],
        )
        ssd_out = ssd_forward(hsize, ssd_args)

        w_b, z_own_part, z_other = call(
            functools.partial(front_kernel, depth, dp, rows),
            [((dp * rows, DI), bf16), ((count, inner), f32), ((count, inner), bf16)],
            (at_b, *slots_b, normed_k),
            5.0,
            scratch=[pltpu.SemaphoreType.DMA((dp,))],
            tables=1,
            raw=dp,
        )
        span = n_out * rows
        held = [pltpu.VMEM((4, span, D), bf16)]
        dg_own, dg_other = call(
            functools.partial(gate_grad_kernel, base, rows),
            [((count, inner), f32), ((count, inner), bf16)],
            (table, w_b, w_a, cot),
            5.0,
            scratch=held + [pltpu.VMEM((DI + rows + 8, count), f32), pltpu.SemaphoreType.DMA((4,))],
            tables=1,
            raw=2,
        )
        gate_in = (z_own_part + swap(z_other).astype(f32)).astype(bf16).astype(f32)
        d_gated = dg_own + swap(dg_other).astype(f32)

        gain = own_seq(gate_g, 0)[None, :]
        sig = jax.nn.sigmoid(gate_in)
        swish = gate_in * sig
        gated = ssd_out * swish
        weighted = d_gated * gain
        sums = jnp.stack([jnp.sum(gated * gated, axis=1), jnp.sum(weighted * gated, axis=1)])
        sums = sums + swap(sums)
        g_scale = lax.rsqrt(sums[0] / DI + norm_eps)[:, None]
        cross = (sums[1] / DI)[:, None]
        gn_own = (gated * g_scale * gain).astype(bf16)
        d_gate_g = jnp.sum(d_gated * gated * g_scale, axis=0)
        d_pre = g_scale * weighted - gated * g_scale**3 * cross
        d_ssd = d_pre * swish
        dz_own = (d_pre * ssd_out * (sig + swish * (1.0 - sig))).astype(bf16)
        gn_own, dz_own, d_ssd = lax.optimization_barrier((gn_own, dz_own, d_ssd))
        gn_other = swap(gn_own)
        dz_other = swap(dz_own)

        d_x, d_bcpre, d_dtraw, d_wx, d_bx, d_wb, d_bb, d_head, d_skip = ssd_backward(
            hsize, ssd_args + (jax.nn.sigmoid(dt_in), d_ssd)
        )
        d_alog, d_dtbias = d_head[0], d_head[1]
        d_skip = jnp.sum(d_skip.reshape(-1, hsize), axis=1)

        gn_k = call(
            functools.partial(pick_kernel, rows),
            [((4, span, count), bf16)],
            (table, gn_own, gn_other),
            3.0,
            scratch=[pltpu.VMEM((DI + rows + 8, count), f32)],
            tables=1,
        )[0]
        d_b = jnp.concatenate([dz_own, dz_other], axis=1)
        parts_b = call(
            functools.partial(weight_grad_kernel, depth, base, 0),
            [((dp * rows, DI), bf16)],
            (normed_k, d_b, gn_k, cot),
            5.0,
        )[0]
        grad_b, _ = scatter_dp(parts_b)

        bcdt_own = jnp.concatenate([d_bcpre, d_dtraw], axis=1).astype(bf16)
        dx_other, bcdt_other = swap(d_x), swap(bcdt_own)
        dx_other, bcdt_other, _ = lax.optimization_barrier((dx_other, bcdt_other, parts_b))
        d_bc = (bcdt_own[:, : 2 * N].astype(f32) + bcdt_other[:, : 2 * N].astype(f32)).astype(bf16)
        dt_pair = jnp.where(
            first,
            jnp.concatenate([bcdt_own[:, 2 * N :], bcdt_other[:, 2 * N :]], axis=1),
            jnp.concatenate([bcdt_other[:, 2 * N :], bcdt_own[:, 2 * N :]], axis=1),
        )
        blank = jnp.zeros((count, WIDE - PROJ), bf16)
        d_a = jnp.concatenate([d_x, dx_other, d_bc, dt_pair, blank], axis=1)
        parts_a = call(
            functools.partial(weight_grad_kernel, depth, base, 2),
            [((dp * rows, 2 * D + side), bf16)],
            (normed_k, d_a, gn_k, cot),
            5.0,
        )[0]
        grad_a, marks_a = scatter_dp(parts_a)

        d_normed = call(
            functools.partial(input_grad_kernel, depth),
            [((count, D), f32)],
            (d_b, tie(d_a, parts_a), w_b, w_a, pick_in),
            5.0,
        )[0]

        d_norm_g = jnp.sum(d_normed * wide * scale, axis=0)

        def spread(a, width):
            full = jnp.zeros(a.shape[:-1] + (width,), f32)
            start = (0,) * (a.ndim - 1) + (s * a.shape[-1],)
            return lax.dynamic_update_slice(full, a, start)

        small_grad = jnp.concatenate(
            [
                jnp.concatenate([spread(d_wx, DI), d_wb], axis=1).reshape(-1),
                spread(d_bx[0], DI),
                d_bb[0],
                d_norm_g,
                spread(d_gate_g, DI),
                spread(d_alog, H),
                spread(d_dtbias, H),
                spread(d_skip, H),
            ]
        )
        small_grad = jnp.pad(small_grad, (0, -SMALL % D)).reshape(-1, D)
        small_grad = sum_all(small_grad, marks_a).reshape(-1)[:SMALL]

        y_part = call(
            functools.partial(out_kernel, base),
            [((count, D), f32)],
            (w_b, w_a, tie(gn_k, d_normed)),
            4.0,
            scratch=held + [pltpu.SemaphoreType.DMA((4,))],
            raw=2,
        )[0]

        def own_tokens(a):
            half = count // 2
            low, high = a[:half], a[half:]
            got = swap(jnp.where(first, high, low).astype(bf16))
            return jnp.where(first, low, high) + got.astype(f32)

        d_own = own_tokens(d_normed)
        y_own = own_tokens(y_part) + x_own.astype(f32)
        wide_own = x_own.astype(f32)
        scale_own = lax.rsqrt(jnp.mean(wide_own * wide_own, axis=-1, keepdims=True) + norm_eps)
        a_own = d_own * norm_g[None, :]
        d_wide = scale_own * a_own - wide_own * scale_own**3 * jnp.mean(
            a_own * wide_own, axis=-1, keepdims=True
        )
        input_grad = (cot_own.astype(f32) + d_wide).astype(bf16)

        def unflip(a, cut):
            keep = k > plan.mix
            if plan.mix_out:
                keep = keep | ((k == plan.mix) & (jnp.arange(rows) >= plan.mix_in)[:, None])
            return jnp.where(keep, a, flip(a, cut))

        grad_a, grad_b = grad_a.astype(f32), grad_b.astype(f32)
        grad_chunk = jnp.concatenate(
            [unflip(grad_b, inner), unflip(grad_a[:, : 2 * D], inner), grad_a[:, 2 * D :]], axis=1
        )
        shard = plan.unpack(grad_chunk, k)
        wing = jnp.pad(small_grad, (flat, flat))
        shard = shard + lax.dynamic_slice(wing, (jnp.clip(flat - at, 0, flat + SMALL),), (flat,))
        updated, first_new, second_new = adamw(params, shard, moment_one, moment_two)
        return (y_own.astype(bf16)[None], input_grad[None], shard, updated, first_new, second_new)

    return on_device


def make(dp, seq):
    def on_device(x_in, cotangent, params, moment_one, moment_two):
        flat = params.shape[0]
        if seq == 2 and small_fits(dp, Plan(dp, seq, flat)):
            return make_pair(dp, flat)(x_in, cotangent, params, moment_one, moment_two)
        return make_general(dp, seq)(x_in, cotangent, params, moment_one, moment_two)

    return on_device


def solution(mesh):
    return jax.shard_map(
        make(mesh.shape["dp"], mesh.shape["seq"]),
        mesh=mesh,
        in_specs=(
            P("dp", "seq", None),
            P("dp", "seq", None),
            P(("dp", "seq")),
            P(("dp", "seq")),
            P(("dp", "seq")),
        ),
        out_specs=(
            P("dp", "seq", None),
            P("dp", "seq", None),
            P(("dp", "seq")),
            P(("dp", "seq")),
            P(("dp", "seq")),
            P(("dp", "seq")),
        ),
        check_vma=False,
    )
```

profile of v0, /device:TPU:0, one launch (start us, length us, event | category | flops | bytes accessed | tf_op | source)
XLA Modules:
  0.0 311.9 jit_solution(14037754911981484972)
XLA Ops:
  10.0 8.3 %collective-permute-done.1.refs_5_ = bf16[56,2432]{1,0:T(8,128)(2,1)S(1)} collective-permute-done((bf16[56,2432]{1,0:T(8,128)(2,1)S(1)}, bf16[56,2432]{1,0:T(8,128)(2,1)S(1)}, u32[]{:S(2)}, u32[]{:S(2)}) %collective-permute-start.1) | collective-permute-done | bytes 272416 | tf_op jit(solution)/shard_map/ppermute | solution.py:936
  22.1 5.4 %collective-permute-done.19 = bf16[128,1024]{1,0:T(8,128)(2,1)S(1)} collective-permute-done((bf16[128,1024]{1,0:T(8,128)(2,1)S(1)}, bf16[128,1024]{1,0:T(8,128)(2,1)S(1)}, u32[]{:S(2)}, u32[]{:S(2)}) %collective-permute-start.19) | collective-permute-done | bytes 262176 | tf_op jit(solution)/shard_map/ppermute | solution.py:979
  42.2 4.9 %collective-permute-done.30.refs_15_ = bf16[56,2432]{1,0:T(8,128)(2,1)} collective-permute-done((bf16[56,2432]{1,0:T(8,128)(2,1)}, bf16[56,2432]{1,0:T(8,128)(2,1)}, u32[]{:S(2)}, u32[]{:S(2)}) %collective-permute-start.30) | collective-permute-done | bytes 272416 | tf_op jit(solution)/shard_map/ppermute | solution.py:941
  52.0 6.1 %collective-permute-done.11.refs_9_ = bf16[56,2048]{1,0:T(8,128)(2,1)} collective-permute-done((bf16[56,2048]{1,0:T(8,128)(2,1)}, bf16[56,2048]{1,0:T(8,128)(2,1)}, u32[]{:S(2)}, u32[]{:S(2)}) %collective-permute-start.11) | collective-permute-done | bytes 229408 | tf_op jit(solution)/shard_map/ppermute | solution.py:936
  58.7 11.1 %fusion.42 = bf16[56,384]{1,0:T(8,128)(2,1)S(1)} fusion(bf16[56,2432]{1,0:T(8,128)(2,1)} %collective-permute-done.30.refs_15_, bf16[56,2432]{1,0:T(8,128)(2,1)} %collective-permute-done.31.refs_14_, bf16[56,2432]{1,0:T(8,128)(2,1)} %collective-permute-done.3.refs_13_, bf16[56,2432]{1,0:T(8,128)(2,1)} %collective-permute-done.29.refs_12_, ...), kind=kLoop, calls=%fused_computation.129 | loop fusion | flops 666624 | bytes 731152 | tf_op jit(solution)/shard_map/add | solution.py:1047
  71.4 5.9 %shard_map.119 = (bf16[896,2432]{1,0:T(8,128)(2,1)}, f32[256,1024]{1,0:T(8,128)}, bf16[256,1024]{1,0:T(8,128)(2,1)}, bf16[256,384]{1,0:T(8,128)(2,1)}) custom-call(s32[16]{0:T(128)} %copy-done.32, bf16[56,2432]{1,0:T(8,128)(2,1)} %copy-done.24, bf16[56,2432]{1,0:T(8,128)(2,1)} %copy-done.19, bf16[56,2432]{1,0:T(8,128)(2,1)} %collective-permute-done.22.refs_2_, ...), custom_call_target="tpu_custom_call" | custom-call | flops 2500000000 | bytes 10000000 | tf_op jit(solution)/shard_map/pallas_call | solution.py:766
  79.1 5.0 %collective-permute-done.33 = bf16[256,384]{1,0:T(8,128)(2,1)S(1)} collective-permute-done((bf16[256,384]{1,0:T(8,128)(2,1)}, bf16[256,384]{1,0:T(8,128)(2,1)S(1)}, u32[]{:S(2)}, u32[]{:S(2)}) %collective-permute-start.33) | collective-permute-done | bytes 196640 | tf_op jit(solution)/shard_map/ppermute | solution.py:979
  95.4 5.6 %shard_map.118 = (bf16[896,2048]{1,0:T(8,128)(2,1)}, f32[256,1024]{1,0:T(8,128)}, bf16[256,1024]{1,0:T(8,128)(2,1)}) custom-call(s32[16]{0:T(128)} %copy-done.32, bf16[56,2048]{1,0:T(8,128)(2,1)} %collective-permute-done.4.refs_0_, bf16[56,2048]{1,0:T(8,128)(2,1)} %copy-done.20, bf16[56,2048]{1,0:T(8,128)(2,1)} %copy-done.34, ...), custom_call_target="tpu_custom_call" | custom-call | flops 2500000000 | bytes 10000000 | tf_op jit(solution)/shard_map/pallas_call | solution.py:766
  101.7 6.2 %shard_map.120 = (f32[256,1024]{1,0:T(8,128)}, bf16[256,1024]{1,0:T(8,128)(2,1)}) custom-call(s32[72]{0:T(128)} %fusion.60.tab_ref, bf16[896,2048]{1,0:T(8,128)(2,1)} %get-tuple-element.42.wb_ref, bf16[896,2432]{1,0:T(8,128)(2,1)} %get-tuple-element.43.wa_ref, bf16[256,1024]{1,0:T(8,128)(2,1)} %pad_maximum_fusion.3.cot_ref), custom_call_target="tpu_custom_call" | custom-call | flops 2500000000 | bytes 10000000 | tf_op jit(solution)/shard_map/pallas_call | solution.py:766
  112.5 4.7 %ssd_forward.1 = f32[256,1024]{1,0:T(8,128)} custom-call(bf16[256,1024]{1,0:T(8,128)(2,1)} %add_convert_fusion.1.x_ref, bf16[256,256]{1,0:T(8,128)(2,1)} %slice.655.bc_ref, f32[4,1024]{1,0:T(4,128)} %constant_dynamic-slice_fusion.wx_ref, f32[1,1024]{1,0:T(1,128)} %bitcast.149, f32[4,256]{1,0:T(4,128)} %slice.508.wb_ref, f32[1,256]{1,0:T(1,128)} %bitcast.154, ...), custom_call_target="tpu_custom_call" | custom-call | flops 2500000000 | bytes 10000000 | tf_op jit(solution)/shard_map/ssd_forward/pallas_call | solution.py:309
  118.8 10.6 %collective-permute-done.36 = bf16[256,1024]{1,0:T(8,128)(2,1)S(1)} collective-permute-done((bf16[256,1024]{1,0:T(8,128)(2,1)}, bf16[256,1024]{1,0:T(8,128)(2,1)S(1)}, u32[]{:S(2)}, u32[]{:S(2)}) %collective-permute-start.36) | collective-permute-done | bytes 524320 | tf_op jit(solution)/shard_map/ppermute | solution.py:979
  138.9 12.1 %ssd_backward.1 = (bf16[256,1024]{1,0:T(8,128)(2,1)}, f32[256,256]{1,0:T(8,128)}, f32[256,16]{1,0:T(8,128)}, f32[4,1024]{1,0:T(4,128)}, f32[1,1024]{1,0:T(1,128)...) custom-call(bf16[256,1024]{1,0:T(8,128)(2,1)} %add_convert_fusion.1.x_ref, ...), custom_call_target="tpu_custom_call" | custom-call | flops 6000000000 | bytes 24000000 | tf_op jit(solution)/shard_map/ssd_backward/pallas_call | solution.py:334
  163.8 16.5 %collective-permute-done.38.other_ref = bf16[256,1024]{1,0:T(8,128)(2,1)} collective-permute-done((bf16[256,1024]{1,0:T(8,128)(2,1)}, bf16[256,1024]{1,0:T(8,128)(2,1)}, u32[]{:S(2)}, u32[]{:S(2)}) %collective-permute-start.38) | collective-permute-done | bytes 524320 | tf_op jit(solution)/shard_map/ppermute | solution.py:979
  183.2 4.7 %shard_map.122 = bf16[896,2048]{1,0:T(8,128)(2,1)} custom-call(bf16[256,616]{1,0:T(8,128)(2,1)} %fusion.5.refs_16_.nk_ref, bf16[256,2048]{1,0:T(8,128)(2,1)} %copy-done.6, bf16[4,336,256]{2,1,0:T(8,128)(2,1)} %shard_map.121.gk_ref, bf16[256,1024]{1,0:T(8,128)(2,1)} %pad_maximum_fusion.3.cot_ref), custom_call_target="tpu_custom_call" | custom-call | flops 2500000000 | bytes 10000000 | tf_op jit(solution)/shard_map/pallas_call | solution.py:766
  193.1 5.2 %shard_map.123 = bf16[896,2432]{1,0:T(8,128)(2,1)} custom-call(bf16[256,616]{1,0:T(8,128)(2,1)} %fusion.5.refs_16_.nk_ref, bf16[256,2432]{1,0:T(8,128)(2,1)} %concatenate.77.d_ref.da_ref, bf16[4,336,256]{2,1,0:T(8,128)(2,1)} %shard_map.121.gk_ref, bf16[256,1024]{1,0:T(8,128)(2,1)} %pad_maximum_fusion.3.cot_ref), custom_call_target="tpu_custom_call" | custom-call | flops 2500000000 | bytes 10000000 | tf_op jit(solution)/shard_map/pallas_call | solution.py:766
  202.0 7.9 %shard_map.124 = f32[256,1024]{1,0:T(8,128)} custom-call(bf16[256,2048]{1,0:T(8,128)(2,1)} %copy-done.6, bf16[256,2432]{1,0:T(8,128)(2,1)} %concatenate.77.d_ref.da_ref, bf16[896,2048]{1,0:T(8,128)(2,1)} %get-tuple-element.42.wb_ref, bf16[896,2432]{1,0:T(8,128)(2,1)} %get-tuple-element.43.wa_ref, bf16[1024,616]{1,0:T(8,128)(2,1)} %fusion.2.pick_ref), custom_call_target="tpu_custom_call" | custom-call | flops 2500000000 | bytes 10000000 | tf_op jit(solution)/shard_map/pallas_call | solution.py:766
  213.6 4.8 %shard_map.125 = f32[256,1024]{1,0:T(8,128)} custom-call(bf16[896,2048]{1,0:T(8,128)(2,1)} %get-tuple-element.42.wb_ref, bf16[896,2432]{1,0:T(8,128)(2,1)} %get-tuple-element.43.wa_ref, bf16[4,336,256]{2,1,0:T(8,128)(2,1)} %shard_map.121.gk_ref), custom_call_target="tpu_custom_call" | custom-call | flops 2000000000 | bytes 8000000 | tf_op jit(solution)/shard_map/pallas_call | solution.py:766
  223.0 5.6 %collective-permute-done.42 = bf16[128,1024]{1,0:T(8,128)(2,1)S(1)} collective-permute-done((bf16[128,1024]{1,0:T(8,128)(2,1)S(1)}, bf16[128,1024]{1,0:T(8,128)(2,1)S(1)}, u32[]{:S(2)}, u32[]{:S(2)}) %collective-permute-start.42) | collective-permute-done | bytes 262176 | tf_op jit(solution)/shard_map/ppermute | solution.py:979
  239.1 14.8 %collective-permute-done.45 = bf16[56,2048]{1,0:T(8,128)(2,1)S(1)} collective-permute-done((bf16[56,2048]{1,0:T(8,128)(2,1)S(1)}, bf16[56,2048]{1,0:T(8,128)(2,1)S(1)}, u32[]{:S(2)}, u32[]{:S(2)}) %collective-permute-start.45) | collective-permute-done | bytes 229408 | tf_op jit(solution)/shard_map/ppermute | solution.py:967
  254.5 6.6 %collective-permute-done.53 = bf16[56,2432]{1,0:T(8,128)(2,1)S(1)} collective-permute-done((bf16[56,2432]{1,0:T(8,128)(2,1)S(1)}, bf16[56,2432]{1,0:T(8,128)(2,1)S(1)}, u32[]{:S(2)}, u32[]{:S(2)}) %collective-permute-start.53) | collective-permute-done | bytes 272416 | tf_op jit(solution)/shard_map/ppermute | solution.py:967
  263.5 5.3 %collective-permute-done.46 = bf16[56,2048]{1,0:T(8,128)(2,1)S(1)} collective-permute-done((bf16[56,2048]{1,0:T(8,128)(2,1)S(1)}, bf16[56,2048]{1,0:T(8,128)(2,1)S(1)}, u32[]{:S(2)}, u32[]{:S(2)}) %collective-permute-start.46) | collective-permute-done | bytes 229408 | tf_op jit(solution)/shard_map/ppermute | solution.py:974
  271.4 5.8 %collective-permute-done.54 = bf16[56,2432]{1,0:T(8,128)(2,1)S(1)} collective-permute-done((bf16[56,2432]{1,0:T(8,128)(2,1)S(1)}, bf16[56,2432]{1,0:T(8,128)(2,1)S(1)}, u32[]{:S(2)}, u32[]{:S(2)}) %collective-permute-start.54) | collective-permute-done | bytes 272416 | tf_op jit(solution)/shard_map/ppermute | solution.py:974
  280.7 5.2 %collective-permute-done.48 = bf16[56,2048]{1,0:T(8,128)(2,1)S(1)} collective-permute-done((bf16[56,2048]{1,0:T(8,128)(2,1)S(1)}, bf16[56,2048]{1,0:T(8,128)(2,1)S(1)}, u32[]{:S(2)}, u32[]{:S(2)}) %collective-permute-start.48) | collective-permute-done | bytes 229408 | tf_op jit(solution)/shard_map/ppermute | solution.py:974
  286.3 5.2 %collective-permute-done.63 = f32[15,1024]{1,0:T(8,128)S(1)} collective-permute-done((f32[15,1024]{1,0:T(8,128)S(1)}, f32[15,1024]{1,0:T(8,128)S(1)}, u32[]{:S(2)}, u32[]{:S(2)}) %collective-permute-start.63) | collective-permute-done | bytes 61472 | tf_op jit(solution)/shard_map/ppermute | solution.py:990
  (354 shorter events, 136.2 us)
Async XLA Ops:
  18.9 13.4 %collective-permute-start.35 = (bf16[128,1024]{1,0:T(8,128)(2,1)S(1)}, bf16[128,1024]{1,0:T(8,128)(2,1)S(1)}, u32[]{:S(2)}, u32[]{:S(2)}) collective-permute-start(bf16[128,1024]{1,0:T(8,128)(2,1)S(1)} %bitcast.140), channel_id=1, source_target_pairs={{0,1},{1,0},{2,3},{3,2},{4,5},{5,4},{6,7},{7,6},{8,9},{9,8},{10,11... | collective-permute-start | bytes 786440 | tf_op jit(solution)/shard_map/ppermute | solution.py:979
  38.1 11.7 %collective-permute-start.26 = (bf16[56,2432]{1,0:T(8,128)(2,1)S(1)}, bf16[56,2432]{1,0:T(8,128)(2,1)S(1)}, u32[]{:S(2)}, u32[]{:S(2)}) collective-permute-start(bf16[56,2432]{1,0:T(8,128)(2,1)S(1)} %collective-permute-done.2.refs_9_), channel_id=1, source_target_pairs={{0,2},{2,0},{4,6},{6,4},{8,10},{10,8},{12,14},{14,12},{16,18},{18,... | collective-permute-start | bytes 817160 | tf_op jit(solution)/shard_map/ppermute | solution.py:943
  38.2 12.2 %collective-permute-start.29 = (bf16[56,2432]{1,0:T(8,128)(2,1)}, bf16[56,2432]{1,0:T(8,128)(2,1)}, u32[]{:S(2)}, u32[]{:S(2)}) collective-permute-start(bf16[56,2432]{1,0:T(8,128)(2,1)} %collective-permute-done.3.refs_13_), channel_id=1, source_target_pairs={{0,2},{2,0},{4,6},{6,4},{8,10},{10,8},{12,14},{14,12},{16,18},{18,... | collective-permute-start | bytes 817160 | tf_op jit(solution)/shard_map/ppermute | solution.py:943
  49.8 28.2 %collective-permute-start.5 = (bf16[56,2048]{1,0:T(8,128)(2,1)S(1)}, bf16[56,2048]{1,0:T(8,128)(2,1)}, u32[]{:S(2)}, u32[]{:S(2)}) collective-permute-start(bf16[56,2048]{1,0:T(8,128)(2,1)S(1)} %get-tuple-element.39.refs_1_), channel_id=1, source_target_pairs={{0,4},{2,6},{4,0},{6,2},{8,12},{10,14},{12,8},{14,10},{16,20},{18,... | collective-permute-start | bytes 688136 | tf_op jit(solution)/shard_map/ppermute | solution.py:941
  50.4 27.6 %collective-permute-start.4 = (bf16[56,2048]{1,0:T(8,128)(2,1)S(1)}, bf16[56,2048]{1,0:T(8,128)(2,1)}, u32[]{:S(2)}, u32[]{:S(2)}) collective-permute-start(bf16[56,2048]{1,0:T(8,128)(2,1)S(1)} %get-tuple-element.39.refs_1_), channel_id=1, source_target_pairs={{0,2},{2,0},{4,6},{6,4},{8,10},{10,8},{12,14},{14,12},{16,18},{18,... | collective-permute-start | bytes 688136 | tf_op jit(solution)/shard_map/ppermute | solution.py:943
  50.4 38.7 %collective-permute-start.9 = (bf16[56,2048]{1,0:T(8,128)(2,1)}, bf16[56,2048]{1,0:T(8,128)(2,1)}, u32[]{:S(2)}, u32[]{:S(2)}) collective-permute-start(bf16[56,2048]{1,0:T(8,128)(2,1)} %collective-permute-done.7.refs_5_), channel_id=1, source_target_pairs={{0,4},{2,6},{4,0},{6,2},{8,12},{10,14},{12,8},{14,10},{16,20},{18,... | collective-permute-start | bytes 688136 | tf_op jit(solution)/shard_map/ppermute | solution.py:941
  58.2 20.4 %collective-permute-start.15 = (bf16[56,2048]{1,0:T(8,128)(2,1)}, bf16[56,2048]{1,0:T(8,128)(2,1)}, u32[]{:S(2)}, u32[]{:S(2)}) collective-permute-start(bf16[56,2048]{1,0:T(8,128)(2,1)} %collective-permute-done.11.refs_9_), channel_id=1, source_target_pairs={{0,8},{2,10},{4,12},{6,14},{8,16},{10,18},{12,20},{14,22},{16,24},... | collective-permute-start | bytes 688136 | tf_op jit(solution)/shard_map/ppermute | solution.py:936
  92.4 19.2 %collective-permute-start.32 = (bf16[256,1024]{1,0:T(8,128)(2,1)}, bf16[256,1024]{1,0:T(8,128)(2,1)S(1)}, u32[]{:S(2)}, u32[]{:S(2)}) collective-permute-start(bf16[256,1024]{1,0:T(8,128)(2,1)} %get-tuple-element.45), channel_id=1, source_target_pairs={{0,1},{1,0},{2,3},{3,2},{4,5},{5,4},{6,7},{7,6},{8,9},{9,8},{10,11... | collective-permute-start | bytes 1572872 | tf_op jit(solution)/shard_map/ppermute | solution.py:979
  101.0 17.8 %collective-permute-start.34 = (bf16[256,1024]{1,0:T(8,128)(2,1)}, bf16[256,1024]{1,0:T(8,128)(2,1)}, u32[]{:S(2)}, u32[]{:S(2)}) collective-permute-start(bf16[256,1024]{1,0:T(8,128)(2,1)} %get-tuple-element.49), channel_id=1, source_target_pairs={{0,1},{1,0},{2,3},{3,2},{4,5},{5,4},{6,7},{7,6},{8,9},{9,8},{10,11... | collective-permute-start | bytes 1572872 | tf_op jit(solution)/shard_map/ppermute | solution.py:979
  107.8 21.6 %collective-permute-start.36 = (bf16[256,1024]{1,0:T(8,128)(2,1)}, bf16[256,1024]{1,0:T(8,128)(2,1)S(1)}, u32[]{:S(2)}, u32[]{:S(2)}) collective-permute-start(bf16[256,1024]{1,0:T(8,128)(2,1)} %get-tuple-element.52), channel_id=1, source_target_pairs={{0,1},{1,0},{2,3},{3,2},{4,5},{5,4},{6,7},{7,6},{8,9},{9,8},{10,11... | collective-permute-start | bytes 1572872 | tf_op jit(solution)/shard_map/ppermute | solution.py:979
  137.4 25.3 %collective-permute-start.39 = (bf16[256,1024]{1,0:T(8,128)(2,1)S(1)}, bf16[256,1024]{1,0:T(8,128)(2,1)}, u32[]{:S(2)}, u32[]{:S(2)}) collective-permute-start(bf16[256,1024]{1,0:T(8,128)(2,1)S(1)} %get-tuple-element.54), channel_id=1, source_target_pairs={{0,1},{1,0},{2,3},{3,2},{4,5},{5,4},{6,7},{7,6},{8,9},{9,8},{10,11... | collective-permute-start | bytes 1572872 | tf_op jit(solution)/shard_map/ppermute | solution.py:979
  154.6 33.3 %collective-permute-start.40 = (bf16[256,1024]{1,0:T(8,128)(2,1)}, bf16[256,1024]{1,0:T(8,128)(2,1)S(1)}, u32[]{:S(2)}, u32[]{:S(2)}) collective-permute-start(bf16[256,1024]{1,0:T(8,128)(2,1)} %get-tuple-element.56), channel_id=1, source_target_pairs={{0,1},{1,0},{2,3},{3,2},{4,5},{5,4},{6,7},{7,6},{8,9},{9,8},{10,11... | collective-permute-start | bytes 1572872 | tf_op jit(solution)/shard_map/ppermute | solution.py:979
  155.2 25.1 %collective-permute-start.38 = (bf16[256,1024]{1,0:T(8,128)(2,1)}, bf16[256,1024]{1,0:T(8,128)(2,1)}, u32[]{:S(2)}, u32[]{:S(2)}) collective-permute-start(bf16[256,1024]{1,0:T(8,128)(2,1)} %get-tuple-element.53.own_ref), channel_id=1, source_target_pairs={{0,1},{1,0},{2,3},{3,2},{4,5},{5,4},{6,7},{7,6},{8,9},{9,8},{10,11... | collective-permute-start | bytes 1572872 | tf_op jit(solution)/shard_map/ppermute | solution.py:979
  160.7 27.2 %collective-permute-start.41 = (bf16[256,272]{1,0:T(8,128)(2,1)}, bf16[256,272]{1,0:T(8,128)(2,1)S(1)}, u32[]{:S(2)}, u32[]{:S(2)}) collective-permute-start(bf16[256,272]{1,0:T(8,128)(2,1)} %pad_maximum_fusion.6), channel_id=1, source_target_pairs={{0,1},{1,0},{2,3},{3,2},{4,5},{5,4},{6,7},{7,6},{8,9},{9,8},{10,11... | collective-permute-start | bytes 417800 | tf_op jit(solution)/shard_map/ppermute | solution.py:979
  191.1 38.6 %collective-permute-start.44 = (bf16[4,2,56,2048]{3,2,1,0:T(8,128)(2,1)}, bf16[4,2,56,2048]{3,2,1,0:T(8,128)(2,1)}, u32[]{:S(2)}, u32[]{:S(2)}) collective-permute-start(bf16[4,2,56,2048]{3,2,1,0:T(8,128)(2,1)} %dynamic-slice_bitcast_fusion.1), channel_id=1, source_target_pairs={{0,2},{2,0},{4,6},{6,4},{8,10},{10,8},{12,14},{14,12},{16,18},{18,... | collective-permute-start | bytes 5505032 | tf_op jit(solution)/shard_map/ppermute | solution.py:957
  201.5 33.2 %collective-permute-start.52 = (bf16[4,2,56,2432]{3,2,1,0:T(8,128)(2,1)}, bf16[4,2,56,2432]{3,2,1,0:T(8,128)(2,1)}, u32[]{:S(2)}, u32[]{:S(2)}) collective-permute-start(bf16[4,2,56,2432]{3,2,1,0:T(8,128)(2,1)} %dynamic-slice_bitcast_fusion), channel_id=1, source_target_pairs={{0,2},{2,0},{4,6},{6,4},{8,10},{10,8},{12,14},{14,12},{16,18},{18,... | collective-permute-start | bytes 6537224 | tf_op jit(solution)/shard_map/ppermute | solution.py:957
  220.9 48.3 %collective-permute-start.62 = (f32[15,1024]{1,0:T(8,128)S(1)}, f32[15,1024]{1,0:T(8,128)S(1)}, u32[]{:S(2)}, u32[]{:S(2)}) collective-permute-start(f32[15,1024]{1,0:T(8,128)S(1)} %add.910), channel_id=1, source_target_pairs={{0,8},{2,10},{4,12},{6,14},{8,0},{10,2},{12,4},{14,6},{16,24},{18,... | collective-permute-start | bytes 184328 | tf_op jit(solution)/shard_map/ppermute | solution.py:990
  232.0 63.7 %collective-permute-start.51 = (bf16[56,2048]{1,0:T(8,128)(2,1)S(1)}, bf16[56,2048]{1,0:T(8,128)(2,1)S(1)}, u32[]{:S(2)}, u32[]{:S(2)}) collective-permute-start(bf16[56,2048]{1,0:T(8,128)(2,1)S(1)} %get-tuple-element.88), channel_id=1, source_target_pairs={{0,4},{2,6},{4,0},{6,2},{8,12},{10,14},{12,8},{14,10},{16,20},{18,... | collective-permute-start | bytes 688136 | tf_op jit(solution)/shard_map/ppermute | solution.py:967
  232.6 44.7 %collective-permute-start.49 = (bf16[56,2048]{1,0:T(8,128)(2,1)S(1)}, bf16[56,2048]{1,0:T(8,128)(2,1)S(1)}, u32[]{:S(2)}, u32[]{:S(2)}) collective-permute-start(bf16[56,2048]{1,0:T(8,128)(2,1)S(1)} %get-tuple-element.89), channel_id=1, source_target_pairs={{0,4},{2,6},{4,0},{6,2},{8,12},{10,14},{12,8},{14,10},{16,20},{18,... | collective-permute-start | bytes 688136 | tf_op jit(solution)/shard_map/ppermute | solution.py:967
  234.1 28.8 %collective-permute-start.47 = (bf16[56,2048]{1,0:T(8,128)(2,1)S(1)}, bf16[56,2048]{1,0:T(8,128)(2,1)S(1)}, u32[]{:S(2)}, u32[]{:S(2)}) collective-permute-start(bf16[56,2048]{1,0:T(8,128)(2,1)S(1)} %get-tuple-element.90), channel_id=1, source_target_pairs={{0,4},{2,6},{4,0},{6,2},{8,12},{10,14},{12,8},{14,10},{16,20},{18,... | collective-permute-start | bytes 688136 | tf_op jit(solution)/shard_map/ppermute | solution.py:967
  234.6 19.3 %collective-permute-start.45 = (bf16[56,2048]{1,0:T(8,128)(2,1)S(1)}, bf16[56,2048]{1,0:T(8,128)(2,1)S(1)}, u32[]{:S(2)}, u32[]{:S(2)}) collective-permute-start(bf16[56,2048]{1,0:T(8,128)(2,1)S(1)} %get-tuple-element.91), channel_id=1, source_target_pairs={{0,4},{2,6},{4,0},{6,2},{8,12},{10,14},{12,8},{14,10},{16,20},{18,... | collective-permute-start | bytes 688136 | tf_op jit(solution)/shard_map/ppermute | solution.py:967
  269.2 30.8 %collective-permute-start.59 = (bf16[56,2432]{1,0:T(8,128)(2,1)S(1)}, bf16[56,2432]{1,0:T(8,128)(2,1)}, u32[]{:S(2)}, u32[]{:S(2)}) collective-permute-start(bf16[56,2432]{1,0:T(8,128)(2,1)S(1)} %get-tuple-element.84), channel_id=1, source_target_pairs={{0,4},{2,6},{4,0},{6,2},{8,12},{10,14},{12,8},{14,10},{16,20},{18,... | collective-permute-start | bytes 817160 | tf_op jit(solution)/shard_map/ppermute | solution.py:967
  270.5 21.0 %collective-permute-start.57 = (bf16[56,2432]{1,0:T(8,128)(2,1)S(1)}, bf16[56,2432]{1,0:T(8,128)(2,1)S(1)}, u32[]{:S(2)}, u32[]{:S(2)}) collective-permute-start(bf16[56,2432]{1,0:T(8,128)(2,1)S(1)} %get-tuple-element.85), channel_id=1, source_target_pairs={{0,4},{2,6},{4,0},{6,2},{8,12},{10,14},{12,8},{14,10},{16,20},{18,... | collective-permute-start | bytes 817160 | tf_op jit(solution)/shard_map/ppermute | solution.py:967
  277.3 14.1 %collective-permute-start.63 = (f32[15,1024]{1,0:T(8,128)S(1)}, f32[15,1024]{1,0:T(8,128)S(1)}, u32[]{:S(2)}, u32[]{:S(2)}) collective-permute-start(f32[15,1024]{1,0:T(8,128)S(1)} %add.911), channel_id=1, source_target_pairs={{0,16},{2,18},{4,20},{6,22},{8,24},{10,26},{12,28},{14,30},{16,0},... | collective-permute-start | bytes 184328 | tf_op jit(solution)/shard_map/ppermute | solution.py:990
  (84 other events, 981.1 us)
where the time goes:
time: 318 us; the launch traced here: 312 us
  waiting for transfers between devices  128 us (40%)
  Pallas kernels  60 us (19%)
  starting transfers between devices  48.6 us (15%)
  other arithmetic  43.3 us (14%)
  local copies, waits for them, and re-layouts  28 us (9%)
    ppermute x15, waiting for transfers between devices, swap(): return lax.ppermute(a, 'seq', [(0, 1), (1, 0)])  45.3 us
    pallas_call x8, Pallas kernels, call(): pl.pallas_call(kernel, out_shape=[jax.ShapeDtypeStruct(a, b) for a, b in...  43.2 us
    ppermute x6, waiting for transfers between devices, scatter_dp(): acc = add(lax.ppermute(acc, 'dp', z_next), mid_sum(z - r))  27.6 us
    ppermute x8, waiting for transfers between devices, mid_sum(): acc = lax.ppermute(acc, 'dp', y_next)  22.1 us
    ppermute x15, starting transfers between devices, swap(): return lax.ppermute(a, 'seq', [(0, 1), (1, 0)])  18.2 us
    ppermute x6, waiting for transfers between devices, gather_dp(): cur = lax.ppermute(cur, 'dp', z_next)  17.8 us
    pallas_call x1, Pallas kernels, ssd_backward(): pl.pallas_call(functools.partial(ssd_backward_kernel, hsize), out_shape=[...  12.1 us
    add x1, other arithmetic, on_device(): functools.reduce(jnp.add, [jnp.where(mine[i], a[:, 2 * D:], 0) for i, a i...  11.1 us
  transfers between devices with their start and end apart: 65, of which 24 were waited for; matrix products, arithmetic and copies ran while one was open for 18% of the time, Pallas kernels for 19%

commit v1 on v0

--- a/solution.py
+++ b/solution.py
@@ -792,6 +792,17 @@
         refs[slots + 4][...] = dot(nk, w_ref[:depth, 2 * half :]).astype(bf16)
 
 
+def small_kernel(slots, want, cols, at_ref, *refs):
+    parts, out_ref, sem = refs[:slots], refs[slots], refs[slots + 1]
+    for i, part in enumerate(parts):
+
+        @pl.when(at_ref[i] == want)
+        def _(part=part):
+            copy = pltpu.make_async_copy(part.at[:, pl.ds(cols, out_ref.shape[1])], out_ref, sem)
+            copy.start()
+            copy.wait()
+
+
 def window_mask(rows, low, high):
     at = lax.broadcasted_iota(jnp.int32, (rows, 1), 0)
     return (at >= low) & (at < high)
@@ -906,8 +917,11 @@
     n_in, n_out = plan.j_in, dp - plan.j_out
     depth, base = n_in * rows, plan.j_out * rows
 
+    ring = list(range(0, za, 2)) + list(range(za - 1 - za % 2, 0, -2))
+    seat = [ring.index(z) for z in range(za)]
+
     def place(z, y, c):
-        return ((z % za) * yb + (y % yb)) * cc + (c % cc)
+        return (ring[z % za] * yb + (y % yb)) * cc + (c % cc)
 
     def perm(dz, dy, dc):
         return [
@@ -921,10 +935,13 @@
 
     def position():
         j = lax.axis_index("dp")
-        return j // (yb * cc), (j // cc) % yb, j % cc
+        return jnp.asarray(seat, jnp.int32)[j // (yb * cc)], (j // cc) % yb, j % cc
+
+    def level(z):
+        return jnp.asarray(ring, jnp.int32)[(z + za) % za]
 
     def index(z, y, c):
-        return (((z + za) % za) * yb + (y + yb) % yb) * cc + c % cc
+        return (level(z) * yb + (y + yb) % yb) * cc + c % cc
 
     def gather_dp(chunk):
         z, y, c = position()
@@ -940,7 +957,8 @@
                 if t:
                     beside = lax.ppermute(beside, "dp", y_next)
                 if cc == 2:
-                    slots.append((index(z - r, y - t, c + 1), lax.ppermute(beside, "dp", c_next)))
+                    mate = lax.ppermute(beside, "dp", c_next)
+                    slots.append((index(z - r, y - t, c + 1), mate))
                 slots.append((index(z - r, y - t, c), beside))
         return jnp.stack([at for at, _ in slots]).astype(jnp.int32), [data for _, data in slots], marks
 
@@ -959,7 +977,7 @@
         total = total.reshape(za * yb, rows, -1)
 
         def core_sum(zi, yi):
-            return lax.dynamic_index_in_dim(total, ((zi + za) % za) * yb + (yi + yb) % yb, 0, False)
+            return lax.dynamic_index_in_dim(total, level(zi) * yb + (yi + yb) % yb, 0, False)
 
         def mid_sum(zi):
             acc = core_sum(zi, y - 1)
@@ -971,7 +989,8 @@
         acc = mid_sum(z - 1)
         marks = [acc]
         for r in range(2, za + 1):
-            acc = add(lax.ppermute(acc, "dp", z_next), mid_sum(z - r))
+            acc = lax.ppermute(acc, "dp", z_next)
+            acc = add(acc, mid_sum(z - r))
             marks.append(acc)
         return acc, marks
 
@@ -1043,10 +1062,15 @@
         in_map = lax.dynamic_index_in_dim(jnp.asarray(plan.in_map.reshape(seq, -1)), tie(s, late), 0, False)
         table = lax.dynamic_index_in_dim(jnp.asarray(plan.windows()), s, 0, False)
         pick_in = (jnp.arange(D)[:, None] == in_map[None, :]).astype(bf16)
-        mine = at_a == dp - 1
-        small = functools.reduce(
-            jnp.add, [jnp.where(mine[i], a[:, 2 * D :], 0) for i, a in enumerate(slots_a)]
-        ).reshape(-1)
+        small = call(
+            functools.partial(small_kernel, dp, dp - 1, 2 * D),
+            [((rows, side), bf16)],
+            (at_a, *slots_a),
+            1.0,
+            scratch=[pltpu.SemaphoreType.DMA],
+            tables=1,
+            raw=dp,
+        )[0].reshape(-1)
         pieces = []
         offset = 0
         for length in (K * CONV, CONV, D, DI, H, H, H):

time: 318 us -> 324 us (1.019)
  waiting for transfers between devices: 128 us -> 116 us
  between operations: 2.16 us -> 13.8 us
  starting transfers between devices: 48.6 us -> 59.9 us
  other arithmetic: 43.3 us -> 35.1 us
    add x1 -> x0, other arithmetic: 11.1 us -> none  [on_device(): functools.reduce(jnp.add, [jnp.where(mine[i], a[:, 2 * D:], 0) for i, a i...]
    ppermute x6, starting transfers between devices: 5 us -> 12.8 us  [gather_dp(): cur = lax.ppermute(cur, 'dp', z_next)]
    ppermute x22, waiting for transfers between devices: 27.7 us -> 22.2 us  [the longest x6 22.1 us: scatter_dp(): acc = lax.ppermute(acc, 'dp', z_next)]
    ppermute x6, waiting for transfers between devices: 17.8 us -> 12.5 us  [gather_dp(): cur = lax.ppermute(cur, 'dp', z_next)]
    ppermute x15, waiting for transfers between devices: 45.3 us -> 40.4 us  [swap(): return lax.ppermute(a, 'seq', [(0, 1), (1, 0)])]
    ppermute x4, waiting for transfers between devices: 5.16 us -> 9.92 us  [sum_all(): got = lax.ppermute(a, 'dp', [(i, i ^ step) for i in range(dp)])]
    pallas_call x8 -> x9, Pallas kernels: 43.2 us -> 45.3 us  [call(): pl.pallas_call(kernel, out_shape=[jax.ShapeDtypeStruct(a, b) for a, b in...]
  transfers between devices with their start and end apart: 65 -> 65, of which waited for: 24 -> 20; matrix products, arithmetic and copies ran while one was open for 18% -> 15% of each run, Pallas kernels for 19% -> 20%
where the time goes in v1:
time: 324 us; the launch traced here: 318 us
  waiting for transfers between devices  116 us (36%)
  Pallas kernels  62.1 us (19%)
  starting transfers between devices  59.9 us (18%)
  other arithmetic  35.1 us (11%)
  local copies, waits for them, and re-layouts  29.7 us (9%)
  between operations  13.8 us (4%)
    pallas_call x9, Pallas kernels, call(): pl.pallas_call(kernel, out_shape=[jax.ShapeDtypeStruct(a, b) for a, b in...  45.3 us
    ppermute x15, waiting for transfers between devices, swap(): return lax.ppermute(a, 'seq', [(0, 1), (1, 0)])  40.4 us
    ppermute x6, waiting for transfers between devices, scatter_dp(): acc = lax.ppermute(acc, 'dp', z_next)  22.1 us
    ppermute x8, waiting for transfers between devices, mid_sum(): acc = lax.ppermute(acc, 'dp', y_next)  20.2 us
    ppermute x15, starting transfers between devices, swap(): return lax.ppermute(a, 'seq', [(0, 1), (1, 0)])  16.7 us
    ppermute x6, starting transfers between devices, gather_dp(): cur = lax.ppermute(cur, 'dp', z_next)  12.8 us
    ppermute x6, waiting for transfers between devices, gather_dp(): cur = lax.ppermute(cur, 'dp', z_next)  12.5 us
    pallas_call x1, Pallas kernels, ssd_backward(): pl.pallas_call(functools.partial(ssd_backward_kernel, hsize), out_shape=[...  12.1 us
  transfers between devices with their start and end apart: 65, of which 20 were waited for; matrix products, arithmetic and copies ran while one was open for 15% of the time, Pallas kernels for 20%

profile of v1, /device:TPU:0, one launch (start us, length us, event | category | flops | bytes accessed | tf_op | source)
XLA Modules:
  0.0 317.9 jit_solution(6468864140203412711)
XLA Ops:
  11.7 5.5 %collective-permute-done.1.refs_5_ = bf16[56,2432]{1,0:T(8,128)(2,1)S(1)} collective-permute-done((bf16[56,2432]{1,0:T(8,128)(2,1)S(1)}, bf16[56,2432]{1,0:T(8,128)(2,1)S(1)}, u32[]{:S(2)}, u32[]{:S(2)}) %collective-permute-start.1) | collective-permute-done | bytes 272416 | tf_op jit(solution)/shard_map/ppermute | solution.py:953
  17.2 3.4 %collective-permute-start.2 = (bf16[56,2432]{1,0:T(8,128)(2,1)S(1)}, bf16[56,2432]{1,0:T(8,128)(2,1)S(1)}, u32[]{:S(2)}, u32[]{:S(2)}) collective-permute-start(bf16[56,2432]{1,0:T(8,128)(2,1)S(1)} %collective-permute-done.1.refs_5_), channel_id=1, source_target_pairs={{0,16},{2,18},{4,20},{6,22},{16,24},{18,26},{20,28},{22,30},{24,8}... | collective-permute-start | bytes 817160 | tf_op jit(solution)/shard_map/ppermute | solution.py:953
  25.2 3.4 %collective-permute-start.3 = (bf16[56,2432]{1,0:T(8,128)(2,1)S(1)}, bf16[56,2432]{1,0:T(8,128)(2,1)}, u32[]{:S(2)}, u32[]{:S(2)}) collective-permute-start(bf16[56,2432]{1,0:T(8,128)(2,1)S(1)} %collective-permute-done.2.refs_9_), channel_id=1, source_target_pairs={{0,16},{2,18},{4,20},{6,22},{16,24},{18,26},{20,28},{22,30},{24,8}... | collective-permute-start | bytes 817160 | tf_op jit(solution)/shard_map/ppermute | solution.py:953
  50.0 4.2 %collective-permute-done.27.refs_11_ = bf16[56,2432]{1,0:T(8,128)(2,1)} collective-permute-done((bf16[56,2432]{1,0:T(8,128)(2,1)S(1)}, bf16[56,2432]{1,0:T(8,128)(2,1)}, u32[]{:S(2)}, u32[]{:S(2)}) %collective-permute-start.27) | collective-permute-done | bytes 272416 | tf_op jit(solution)/shard_map/ppermute | solution.py:958
  54.1 5.2 %collective-permute-done.30.refs_15_ = bf16[56,2432]{1,0:T(8,128)(2,1)} collective-permute-done((bf16[56,2432]{1,0:T(8,128)(2,1)}, bf16[56,2432]{1,0:T(8,128)(2,1)}, u32[]{:S(2)}, u32[]{:S(2)}) %collective-permute-start.30) | collective-permute-done | bytes 272416 | tf_op jit(solution)/shard_map/ppermute | solution.py:958
  63.3 4.9 %collective-permute-done.11.refs_9_ = bf16[56,2048]{1,0:T(8,128)(2,1)S(1)} collective-permute-done((bf16[56,2048]{1,0:T(8,128)(2,1)S(1)}, bf16[56,2048]{1,0:T(8,128)(2,1)S(1)}, u32[]{:S(2)}, u32[]{:S(2)}) %collective-permute-start.11) | collective-permute-done | bytes 229408 | tf_op jit(solution)/shard_map/ppermute | solution.py:953
  75.5 5.9 %shard_map.588 = (bf16[896,2432]{1,0:T(8,128)(2,1)}, f32[256,1024]{1,0:T(8,128)}, bf16[256,1024]{1,0:T(8,128)(2,1)}, bf16[256,384]{1,0:T(8,128)(2,1)}) custom-call(s32[16]{0:T(128)} %stack.127.at_ref, bf16[56,2432]{1,0:T(8,128)(2,1)} %copy-done.23, bf16[56,2432]{1,0:T(8,128)(2,1)} %copy-done.8, bf16[56,2432]{1,0:T(8,128)(2,1)} %copy-done.25, ...), custom_call_target="tpu_custom_call" | custom-call | flops 2500000000 | bytes 10000000 | tf_op jit(solution)/shard_map/pallas_call | solution.py:766
  99.4 5.6 %shard_map.587 = (bf16[896,2048]{1,0:T(8,128)(2,1)}, f32[256,1024]{1,0:T(8,128)}, bf16[256,1024]{1,0:T(8,128)(2,1)}) custom-call(s32[16]{0:T(128)} %stack.127.at_ref, bf16[56,2048]{1,0:T(8,128)(2,1)} %copy-done.36, bf16[56,2048]{1,0:T(8,128)(2,1)} %get-tuple-element.39.refs_1_, bf16[56,2048]{1,0:T(8,128)(2,1)} %copy-done.38, bf16[56,2048]{1,0:T(8,128)(2,1)} %copy-done.35, ...), custom_call_target="tpu_custom_call" | custom-call | flops 2500000000 | bytes 10000000 | tf_op jit(solution)/shard_map/pallas_call | solution.py:766
  106.4 6.2 %shard_map.589 = (f32[256,1024]{1,0:T(8,128)}, bf16[256,1024]{1,0:T(8,128)(2,1)}) custom-call(s32[72]{0:T(128)} %fusion.45.tab_ref, bf16[896,2048]{1,0:T(8,128)(2,1)} %get-tuple-element.42.wb_ref, bf16[896,2432]{1,0:T(8,128)(2,1)} %get-tuple-element.43.wa_ref, bf16[256,1024]{1,0:T(8,128)(2,1)} %pad_maximum_fusion.3.cot_ref), custom_call_target="tpu_custom_call" | custom-call | flops 2500000000 | bytes 10000000 | tf_op jit(solution)/shard_map/pallas_call | solution.py:766
  116.5 4.7 %ssd_forward.1 = f32[256,1024]{1,0:T(8,128)} custom-call(bf16[256,1024]{1,0:T(8,128)(2,1)} %add_convert_fusion.1.x_ref, bf16[256,256]{1,0:T(8,128)(2,1)} %slice.435.bc_ref, f32[4,1024]{1,0:T(4,128)} %constant_dynamic-slice_fusion.wx_ref, f32[1,1024]{1,0:T(1,128)} %bitcast.146, f32[4,256]{1,0:T(4,128)} %slice.364.wb_ref, f32[1,256]{1,0:T(1,128)} %bitcast.151, ...), custom_call_target="tpu_custom_call" | custom-call | flops 2500000000 | bytes 10000000 | tf_op jit(solution)/shard_map/ssd_forward/pallas_call | solution.py:309
  124.4 10.7 %collective-permute-done.36 = bf16[256,1024]{1,0:T(8,128)(2,1)S(1)} collective-permute-done((bf16[256,1024]{1,0:T(8,128)(2,1)}, bf16[256,1024]{1,0:T(8,128)(2,1)S(1)}, u32[]{:S(2)}, u32[]{:S(2)}) %collective-permute-start.36) | collective-permute-done | bytes 524320 | tf_op jit(solution)/shard_map/ppermute | solution.py:998
  143.7 12.1 %ssd_backward.1 = (bf16[256,1024]{1,0:T(8,128)(2,1)}, f32[256,256]{1,0:T(8,128)}, f32[256,16]{1,0:T(8,128)}, f32[4,1024]{1,0:T(4,128)}, f32[1,1024]{1,0:T(1,128)...) custom-call(bf16[256,1024]{1,0:T(8,128)(2,1)} %add_convert_fusion.1.x_ref, ...), custom_call_target="tpu_custom_call" | custom-call | flops 6000000000 | bytes 24000000 | tf_op jit(solution)/shard_map/ssd_backward/pallas_call | solution.py:334
  169.3 16.0 %collective-permute-done.38.other_ref = bf16[256,1024]{1,0:T(8,128)(2,1)} collective-permute-done((bf16[256,1024]{1,0:T(8,128)(2,1)}, bf16[256,1024]{1,0:T(8,128)(2,1)}, u32[]{:S(2)}, u32[]{:S(2)}) %collective-permute-start.38) | collective-permute-done | bytes 524320 | tf_op jit(solution)/shard_map/ppermute | solution.py:998
  188.2 4.7 %shard_map.591 = bf16[896,2048]{1,0:T(8,128)(2,1)} custom-call(bf16[256,616]{1,0:T(8,128)(2,1)} %fusion.5.refs_16_.nk_ref, bf16[256,2048]{1,0:T(8,128)(2,1)} %copy-done.6, bf16[4,336,256]{2,1,0:T(8,128)(2,1)} %shard_map.590.gk_ref, bf16[256,1024]{1,0:T(8,128)(2,1)} %pad_maximum_fusion.3.cot_ref), custom_call_target="tpu_custom_call" | custom-call | flops 2500000000 | bytes 10000000 | tf_op jit(solution)/shard_map/pallas_call | solution.py:766
  198.2 5.2 %shard_map.592 = bf16[896,2432]{1,0:T(8,128)(2,1)} custom-call(bf16[256,616]{1,0:T(8,128)(2,1)} %fusion.5.refs_16_.nk_ref, bf16[256,2432]{1,0:T(8,128)(2,1)} %concatenate.77.d_ref.da_ref, bf16[4,336,256]{2,1,0:T(8,128)(2,1)} %shard_map.590.gk_ref, bf16[256,1024]{1,0:T(8,128)(2,1)} %pad_maximum_fusion.3.cot_ref), custom_call_target="tpu_custom_call" | custom-call | flops 2500000000 | bytes 10000000 | tf_op jit(solution)/shard_map/pallas_call | solution.py:766
  207.0 7.9 %shard_map.593 = f32[256,1024]{1,0:T(8,128)} custom-call(bf16[256,2048]{1,0:T(8,128)(2,1)} %copy-done.6, bf16[256,2432]{1,0:T(8,128)(2,1)} %concatenate.77.d_ref.da_ref, bf16[896,2048]{1,0:T(8,128)(2,1)} %get-tuple-element.42.wb_ref, bf16[896,2432]{1,0:T(8,128)(2,1)} %get-tuple-element.43.wa_ref, bf16[1024,616]{1,0:T(8,128)(2,1)} %fusion.2.pick_ref), custom_call_target="tpu_custom_call" | custom-call | flops 2500000000 | bytes 10000000 | tf_op jit(solution)/shard_map/pallas_call | solution.py:766
  218.7 4.8 %shard_map.594 = f32[256,1024]{1,0:T(8,128)} custom-call(bf16[896,2048]{1,0:T(8,128)(2,1)} %get-tuple-element.42.wb_ref, bf16[896,2432]{1,0:T(8,128)(2,1)} %get-tuple-element.43.wa_ref, bf16[4,336,256]{2,1,0:T(8,128)(2,1)} %shard_map.590.gk_ref), custom_call_target="tpu_custom_call" | custom-call | flops 2000000000 | bytes 8000000 | tf_op jit(solution)/shard_map/pallas_call | solution.py:766
  227.0 6.7 %collective-permute-done.42 = bf16[128,1024]{1,0:T(8,128)(2,1)S(1)} collective-permute-done((bf16[128,1024]{1,0:T(8,128)(2,1)S(1)}, bf16[128,1024]{1,0:T(8,128)(2,1)S(1)}, u32[]{:S(2)}, u32[]{:S(2)}) %collective-permute-start.42) | collective-permute-done | bytes 262176 | tf_op jit(solution)/shard_map/ppermute | solution.py:998
  244.1 14.9 %collective-permute-done.45 = bf16[56,2048]{1,0:T(8,128)(2,1)S(1)} collective-permute-done((bf16[56,2048]{1,0:T(8,128)(2,1)S(1)}, bf16[56,2048]{1,0:T(8,128)(2,1)S(1)}, u32[]{:S(2)}, u32[]{:S(2)}) %collective-permute-start.45) | collective-permute-done | bytes 229408 | tf_op jit(solution)/shard_map/ppermute | solution.py:985
  260.8 5.3 %collective-permute-done.53 = bf16[56,2432]{1,0:T(8,128)(2,1)S(1)} collective-permute-done((bf16[56,2432]{1,0:T(8,128)(2,1)S(1)}, bf16[56,2432]{1,0:T(8,128)(2,1)S(1)}, u32[]{:S(2)}, u32[]{:S(2)}) %collective-permute-start.53) | collective-permute-done | bytes 272416 | tf_op jit(solution)/shard_map/ppermute | solution.py:985
  268.3 4.5 %collective-permute-done.46 = bf16[56,2048]{1,0:T(8,128)(2,1)S(1)} collective-permute-done((bf16[56,2048]{1,0:T(8,128)(2,1)S(1)}, bf16[56,2048]{1,0:T(8,128)(2,1)S(1)}, u32[]{:S(2)}, u32[]{:S(2)}) %collective-permute-start.46) | collective-permute-done | bytes 229408 | tf_op jit(solution)/shard_map/ppermute | solution.py:992
  275.7 5.6 %collective-permute-done.54 = bf16[56,2432]{1,0:T(8,128)(2,1)S(1)} collective-permute-done((bf16[56,2432]{1,0:T(8,128)(2,1)S(1)}, bf16[56,2432]{1,0:T(8,128)(2,1)S(1)}, u32[]{:S(2)}, u32[]{:S(2)}) %collective-permute-start.54) | collective-permute-done | bytes 272416 | tf_op jit(solution)/shard_map/ppermute | solution.py:992
  282.4 7.3 %collective-permute-done.48 = bf16[56,2048]{1,0:T(8,128)(2,1)S(1)} collective-permute-done((bf16[56,2048]{1,0:T(8,128)(2,1)S(1)}, bf16[56,2048]{1,0:T(8,128)(2,1)S(1)}, u32[]{:S(2)}, u32[]{:S(2)}) %collective-permute-start.48) | collective-permute-done | bytes 229408 | tf_op jit(solution)/shard_map/ppermute | solution.py:992
  290.9 9.9 %collective-permute-done.63 = f32[15,1024]{1,0:T(8,128)S(1)} collective-permute-done((f32[15,1024]{1,0:T(8,128)S(1)}, f32[15,1024]{1,0:T(8,128)S(1)}, u32[]{:S(2)}, u32[]{:S(2)}) %collective-permute-start.63) | collective-permute-done | bytes 61472 | tf_op jit(solution)/shard_map/ppermute | solution.py:1009
  (356 shorter events, 139.5 us)
Async XLA Ops:
  22.6 21.7 %collective-permute-start.20 = (bf16[56,2432]{1,0:T(8,128)(2,1)S(1)}, bf16[56,2432]{1,0:T(8,128)(2,1)S(1)}, u32[]{:S(2)}, u32[]{:S(2)}) collective-permute-start(bf16[56,2432]{1,0:T(8,128)(2,1)S(1)} %slice_select_fusion.refs_1_), channel_id=1, source_target_pairs={{0,2},{2,0},{4,6},{6,4},{16,18},{18,16},{20,22},{22,20},{24,26},{2... | collective-permute-start | bytes 817160 | tf_op jit(solution)/shard_map/ppermute | solution.py:960
  22.6 24.0 %collective-permute-start.24 = (bf16[56,2432]{1,0:T(8,128)(2,1)S(1)}, bf16[56,2432]{1,0:T(8,128)(2,1)S(1)}, u32[]{:S(2)}, u32[]{:S(2)}) collective-permute-start(bf16[56,2432]{1,0:T(8,128)(2,1)S(1)} %collective-permute-done.1.refs_5_), channel_id=1, source_target_pairs={{0,4},{2,6},{4,0},{6,2},{16,20},{18,22},{20,16},{22,18},{24,28},{2... | collective-permute-start | bytes 817160 | tf_op jit(solution)/shard_map/ppermute | solution.py:958
  25.2 21.5 %collective-permute-start.3 = (bf16[56,2432]{1,0:T(8,128)(2,1)S(1)}, bf16[56,2432]{1,0:T(8,128)(2,1)}, u32[]{:S(2)}, u32[]{:S(2)}) collective-permute-start(bf16[56,2432]{1,0:T(8,128)(2,1)S(1)} %collective-permute-done.2.refs_9_), channel_id=1, source_target_pairs={{0,16},{2,18},{4,20},{6,22},{16,24},{18,26},{20,28},{22,30},{24,8}... | collective-permute-start | bytes 817160 | tf_op jit(solution)/shard_map/ppermute | solution.py:953
  29.7 17.3 %collective-permute-start.22 = (bf16[56,2432]{1,0:T(8,128)(2,1)S(1)}, bf16[56,2432]{1,0:T(8,128)(2,1)S(1)}, u32[]{:S(2)}, u32[]{:S(2)}) collective-permute-start(bf16[56,2432]{1,0:T(8,128)(2,1)S(1)} %collective-permute-done.21.refs_3_), channel_id=1, source_target_pairs={{0,2},{2,0},{4,6},{6,4},{16,18},{18,16},{20,22},{22,20},{24,26},{2... | collective-permute-start | bytes 817160 | tf_op jit(solution)/shard_map/ppermute | solution.py:960
  61.2 22.6 %collective-permute-start.5 = (bf16[56,2048]{1,0:T(8,128)(2,1)}, bf16[56,2048]{1,0:T(8,128)(2,1)S(1)}, u32[]{:S(2)}, u32[]{:S(2)}) collective-permute-start(bf16[56,2048]{1,0:T(8,128)(2,1)} %get-tuple-element.39.refs_1_), channel_id=1, source_target_pairs={{0,4},{2,6},{4,0},{6,2},{16,20},{18,22},{20,16},{22,18},{24,28},{2... | collective-permute-start | bytes 688136 | tf_op jit(solution)/shard_map/ppermute | solution.py:958
  63.0 20.8 %collective-permute-start.4 = (bf16[56,2048]{1,0:T(8,128)(2,1)}, bf16[56,2048]{1,0:T(8,128)(2,1)S(1)}, u32[]{:S(2)}, u32[]{:S(2)}) collective-permute-start(bf16[56,2048]{1,0:T(8,128)(2,1)} %get-tuple-element.39.refs_1_), channel_id=1, source_target_pairs={{0,2},{2,0},{4,6},{6,4},{16,18},{18,16},{20,22},{22,20},{24,26},{2... | collective-permute-start | bytes 688136 | tf_op jit(solution)/shard_map/ppermute | solution.py:960
  63.0 31.9 %collective-permute-start.9 = (bf16[56,2048]{1,0:T(8,128)(2,1)S(1)}, bf16[56,2048]{1,0:T(8,128)(2,1)}, u32[]{:S(2)}, u32[]{:S(2)}) collective-permute-start(bf16[56,2048]{1,0:T(8,128)(2,1)S(1)} %collective-permute-done.7.refs_5_), channel_id=1, source_target_pairs={{0,4},{2,6},{4,0},{6,2},{16,20},{18,22},{20,16},{22,18},{24,28},{2... | collective-permute-start | bytes 688136 | tf_op jit(solution)/shard_map/ppermute | solution.py:958
  98.0 17.6 %collective-permute-start.32 = (bf16[256,1024]{1,0:T(8,128)(2,1)}, bf16[256,1024]{1,0:T(8,128)(2,1)S(1)}, u32[]{:S(2)}, u32[]{:S(2)}) collective-permute-start(bf16[256,1024]{1,0:T(8,128)(2,1)} %get-tuple-element.45), channel_id=1, source_target_pairs={{0,1},{1,0},{2,3},{3,2},{4,5},{5,4},{6,7},{7,6},{8,9},{9,8},{10,11... | collective-permute-start | bytes 1572872 | tf_op jit(solution)/shard_map/ppermute | solution.py:998
  105.0 19.4 %collective-permute-start.34 = (bf16[256,1024]{1,0:T(8,128)(2,1)}, bf16[256,1024]{1,0:T(8,128)(2,1)}, u32[]{:S(2)}, u32[]{:S(2)}) collective-permute-start(bf16[256,1024]{1,0:T(8,128)(2,1)} %get-tuple-element.49), channel_id=1, source_target_pairs={{0,1},{1,0},{2,3},{3,2},{4,5},{5,4},{6,7},{7,6},{8,9},{9,8},{10,11... | collective-permute-start | bytes 1572872 | tf_op jit(solution)/shard_map/ppermute | solution.py:998
  112.6 22.5 %collective-permute-start.36 = (bf16[256,1024]{1,0:T(8,128)(2,1)}, bf16[256,1024]{1,0:T(8,128)(2,1)S(1)}, u32[]{:S(2)}, u32[]{:S(2)}) collective-permute-start(bf16[256,1024]{1,0:T(8,128)(2,1)} %get-tuple-element.52), channel_id=1, source_target_pairs={{0,1},{1,0},{2,3},{3,2},{4,5},{5,4},{6,7},{7,6},{8,9},{9,8},{10,11... | collective-permute-start | bytes 1572872 | tf_op jit(solution)/shard_map/ppermute | solution.py:998
  143.0 25.2 %collective-permute-start.39 = (bf16[256,1024]{1,0:T(8,128)(2,1)S(1)}, bf16[256,1024]{1,0:T(8,128)(2,1)}, u32[]{:S(2)}, u32[]{:S(2)}) collective-permute-start(bf16[256,1024]{1,0:T(8,128)(2,1)S(1)} %get-tuple-element.54), channel_id=1, source_target_pairs={{0,1},{1,0},{2,3},{3,2},{4,5},{5,4},{6,7},{7,6},{8,9},{9,8},{10,11... | collective-permute-start | bytes 1572872 | tf_op jit(solution)/shard_map/ppermute | solution.py:998
  159.3 33.6 %collective-permute-start.40 = (bf16[256,1024]{1,0:T(8,128)(2,1)}, bf16[256,1024]{1,0:T(8,128)(2,1)S(1)}, u32[]{:S(2)}, u32[]{:S(2)}) collective-permute-start(bf16[256,1024]{1,0:T(8,128)(2,1)} %get-tuple-element.56), channel_id=1, source_target_pairs={{0,1},{1,0},{2,3},{3,2},{4,5},{5,4},{6,7},{7,6},{8,9},{9,8},{10,11... | collective-permute-start | bytes 1572872 | tf_op jit(solution)/shard_map/ppermute | solution.py:998
  160.8 24.6 %collective-permute-start.38 = (bf16[256,1024]{1,0:T(8,128)(2,1)}, bf16[256,1024]{1,0:T(8,128)(2,1)}, u32[]{:S(2)}, u32[]{:S(2)}) collective-permute-start(bf16[256,1024]{1,0:T(8,128)(2,1)} %get-tuple-element.53.own_ref), channel_id=1, source_target_pairs={{0,1},{1,0},{2,3},{3,2},{4,5},{5,4},{6,7},{7,6},{8,9},{9,8},{10,11... | collective-permute-start | bytes 1572872 | tf_op jit(solution)/shard_map/ppermute | solution.py:998
  165.4 27.5 %collective-permute-start.41 = (bf16[256,272]{1,0:T(8,128)(2,1)}, bf16[256,272]{1,0:T(8,128)(2,1)S(1)}, u32[]{:S(2)}, u32[]{:S(2)}) collective-permute-start(bf16[256,272]{1,0:T(8,128)(2,1)} %pad_maximum_fusion.6), channel_id=1, source_target_pairs={{0,1},{1,0},{2,3},{3,2},{4,5},{5,4},{6,7},{7,6},{8,9},{9,8},{10,11... | collective-permute-start | bytes 417800 | tf_op jit(solution)/shard_map/ppermute | solution.py:998
  196.2 38.6 %collective-permute-start.44 = (bf16[4,2,56,2048]{3,2,1,0:T(8,128)(2,1)}, bf16[4,2,56,2048]{3,2,1,0:T(8,128)(2,1)}, u32[]{:S(2)}, u32[]{:S(2)}) collective-permute-start(bf16[4,2,56,2048]{3,2,1,0:T(8,128)(2,1)} %dynamic-slice_bitcast_fusion.1), channel_id=1, source_target_pairs={{0,2},{2,0},{4,6},{6,4},{16,18},{18,16},{20,22},{22,20},{24,26},{2... | collective-permute-start | bytes 5505032 | tf_op jit(solution)/shard_map/ppermute | solution.py:975
  206.5 34.4 %collective-permute-start.52 = (bf16[4,2,56,2432]{3,2,1,0:T(8,128)(2,1)}, bf16[4,2,56,2432]{3,2,1,0:T(8,128)(2,1)}, u32[]{:S(2)}, u32[]{:S(2)}) collective-permute-start(bf16[4,2,56,2432]{3,2,1,0:T(8,128)(2,1)} %dynamic-slice_bitcast_fusion), channel_id=1, source_target_pairs={{0,2},{2,0},{4,6},{6,4},{16,18},{18,16},{20,22},{22,20},{24,26},{2... | collective-permute-start | bytes 6537224 | tf_op jit(solution)/shard_map/ppermute | solution.py:975
  226.2 47.3 %collective-permute-start.62 = (f32[15,1024]{1,0:T(8,128)S(1)}, f32[15,1024]{1,0:T(8,128)S(1)}, u32[]{:S(2)}, u32[]{:S(2)}) collective-permute-start(f32[15,1024]{1,0:T(8,128)S(1)} %add.1255), channel_id=1, source_target_pairs={{0,8},{2,10},{4,12},{6,14},{8,0},{10,2},{12,4},{14,6},{16,24},{18,... | collective-permute-start | bytes 184328 | tf_op jit(solution)/shard_map/ppermute | solution.py:1009
  237.1 68.3 %collective-permute-start.51 = (bf16[56,2048]{1,0:T(8,128)(2,1)S(1)}, bf16[56,2048]{1,0:T(8,128)(2,1)S(1)}, u32[]{:S(2)}, u32[]{:S(2)}) collective-permute-start(bf16[56,2048]{1,0:T(8,128)(2,1)S(1)} %get-tuple-element.88), channel_id=1, source_target_pairs={{0,4},{2,6},{4,0},{6,2},{16,20},{18,22},{20,16},{22,18},{24,28},{2... | collective-permute-start | bytes 688136 | tf_op jit(solution)/shard_map/ppermute | solution.py:985
  238.9 43.0 %collective-permute-start.49 = (bf16[56,2048]{1,0:T(8,128)(2,1)S(1)}, bf16[56,2048]{1,0:T(8,128)(2,1)S(1)}, u32[]{:S(2)}, u32[]{:S(2)}) collective-permute-start(bf16[56,2048]{1,0:T(8,128)(2,1)S(1)} %get-tuple-element.89), channel_id=1, source_target_pairs={{0,4},{2,6},{4,0},{6,2},{16,20},{18,22},{20,16},{22,18},{24,28},{2... | collective-permute-start | bytes 688136 | tf_op jit(solution)/shard_map/ppermute | solution.py:985
  239.2 27.3 %collective-permute-start.47 = (bf16[56,2048]{1,0:T(8,128)(2,1)S(1)}, bf16[56,2048]{1,0:T(8,128)(2,1)S(1)}, u32[]{:S(2)}, u32[]{:S(2)}) collective-permute-start(bf16[56,2048]{1,0:T(8,128)(2,1)S(1)} %get-tuple-element.90), channel_id=1, source_target_pairs={{0,4},{2,6},{4,0},{6,2},{16,20},{18,22},{20,16},{22,18},{24,28},{2... | collective-permute-start | bytes 688136 | tf_op jit(solution)/shard_map/ppermute | solution.py:985
  240.9 18.1 %collective-permute-start.45 = (bf16[56,2048]{1,0:T(8,128)(2,1)S(1)}, bf16[56,2048]{1,0:T(8,128)(2,1)S(1)}, u32[]{:S(2)}, u32[]{:S(2)}) collective-permute-start(bf16[56,2048]{1,0:T(8,128)(2,1)S(1)} %get-tuple-element.91), channel_id=1, source_target_pairs={{0,4},{2,6},{4,0},{6,2},{16,20},{18,22},{20,16},{22,18},{24,28},{2... | collective-permute-start | bytes 688136 | tf_op jit(solution)/shard_map/ppermute | solution.py:985
  273.5 33.6 %collective-permute-start.59 = (bf16[56,2432]{1,0:T(8,128)(2,1)S(1)}, bf16[56,2432]{1,0:T(8,128)(2,1)}, u32[]{:S(2)}, u32[]{:S(2)}) collective-permute-start(bf16[56,2432]{1,0:T(8,128)(2,1)S(1)} %get-tuple-element.84), channel_id=1, source_target_pairs={{0,4},{2,6},{4,0},{6,2},{16,20},{18,22},{20,16},{22,18},{24,28},{2... | collective-permute-start | bytes 817160 | tf_op jit(solution)/shard_map/ppermute | solution.py:985
  275.3 25.6 %collective-permute-start.57 = (bf16[56,2432]{1,0:T(8,128)(2,1)S(1)}, bf16[56,2432]{1,0:T(8,128)(2,1)S(1)}, u32[]{:S(2)}, u32[]{:S(2)}) collective-permute-start(bf16[56,2432]{1,0:T(8,128)(2,1)S(1)} %get-tuple-element.85), channel_id=1, source_target_pairs={{0,4},{2,6},{4,0},{6,2},{16,20},{18,22},{20,16},{22,18},{24,28},{2... | collective-permute-start | bytes 817160 | tf_op jit(solution)/shard_map/ppermute | solution.py:985
  281.9 19.0 %collective-permute-start.63 = (f32[15,1024]{1,0:T(8,128)S(1)}, f32[15,1024]{1,0:T(8,128)S(1)}, u32[]{:S(2)}, u32[]{:S(2)}) collective-permute-start(f32[15,1024]{1,0:T(8,128)S(1)} %add.1256), channel_id=1, source_target_pairs={{0,16},{2,18},{4,20},{6,22},{8,24},{10,26},{12,28},{14,30},{16,0},... | collective-permute-start | bytes 184328 | tf_op jit(solution)/shard_map/ppermute | solution.py:1009
  (85 other events, 941.4 us)
